TPU v7x, 512 devices: a whole 4x8x8 slice. The times are simulated.
512 devices in a mesh: gx: 16 (over z, core), gy: 32 (over x, y).
Axes of the slice: x: 4, y: 8, z: 8, core: 2. Of those that a mesh axis runs over, the one named last changes fastest.
Arguments:
- state: float32 [128, 512, 256], P('gx', 'gy'), may hold values from -4 to 4
- forcing: float32 [128, 512, 256], P('gx', 'gy'), may hold values from -24 to 24
Outputs:
- new_state: float32 [128, 512, 256], P('gx', 'gy')
All inputs are finite; a program needn't handle non-finite values.
Results may differ from a plain program's by a relative error of at most 0.0003.
Values sent between devices are 32-bit elements; how exact they have to be, the bound alone decides.
A program may use at most 64 MiB of HBM per device.

v0:
```python
import jax
import jax.numpy as jnp
import numpy as np
from jax import lax
from jax.sharding import PartitionSpec as P

SWEEPS = 6


fine_offsets = [(0, 0, 0), (-1, 0, 0), (1, 0, 0), (0, -1, 0), (0, 1, 0), (0, 0, -1), (0, 0, 1)]
coarse_offsets = [
    (first, second, third) for first in (-1, 0, 1) for second in (-1, 0, 1) for third in (-1, 0, 1)
]
smoothing_weight = 0.6


def with_halo(block, sides, width):
    for axis, dim in sides:
        count = lax.axis_size(axis)
        forward = [(i, i + 1) for i in range(count - 1)]
        forward.append((count - 1, 0))
        backward = [(target, source) for source, target in forward]
        low = lax.ppermute(
            lax.slice_in_dim(block, block.shape[dim] - width, None, axis=dim), axis, forward
        )
        high = lax.ppermute(lax.slice_in_dim(block, 0, width, axis=dim), axis, backward)
        block = jnp.concatenate([low, block, high], axis=dim)
    return block


def from_behind(value, axis, steps):
    count = lax.axis_size(axis)
    pairs = [(source, (source + steps) % count) for source in range(count)]
    return lax.ppermute(value, axis, pairs)


def shifted(value, axis, by):
    devices = lax.axis_size(axis)
    pairs = [(i, i + by) for i in range(devices) if 0 <= i + by < devices]
    return lax.ppermute(value, axis, pairs)


def tap_table():
    table = np.zeros((3, 3, 3), np.float32)
    for fine_step in range(3):
        for coarse_step in range(3):
            for place in range(3):
                spread = abs(place - 1 + (fine_step - 1) - 2 * (coarse_step - 1))
                table[fine_step, coarse_step, place] = (1.0 - abs(place - 1) / 2.0) * max(
                    0.0, 1.0 - spread / 2.0
                )
    return table


def strided_views(field, axis):
    count = field.shape[axis] - 1
    return [
        (
            lax.slice_in_dim(field, start, start + count - 1, 2, axis)
            if start == 0
            else lax.slice_in_dim(field, start, count + 1 if start == 2 else count, 2, axis)
        )
        for start in range(3)
    ]


def coarse_sum(field, axis):
    views = strided_views(field, axis)
    return 0.5 * views[0] + views[1] + 0.5 * views[2]


def alternate(field, axis):
    count = field.shape[axis] - 1
    base = lax.slice_in_dim(field, 0, count, 1, axis)
    following = lax.slice_in_dim(field, 1, count + 1, 1, axis)
    paired = jnp.stack([base, 0.5 * (base + following)], axis + 1)
    shape = list(base.shape)
    shape[axis] = 2 * count
    return paired.reshape(shape)


def edge_masks(first, count, total):
    rows = first + jnp.arange(count, dtype=jnp.int32)
    return jnp.stack(
        [((rows + step >= 0) & (rows + step < total)).astype(jnp.float32) for step in (-1, 0, 1)]
    )


def row_flags(first, count, total):
    rows = first + jnp.arange(count, dtype=jnp.int32)
    interior_flag = ((rows >= 0) & (rows < total)).astype(jnp.float32)
    return (interior_flag, (rows > 0).astype(jnp.float32), (rows < total - 1).astype(jnp.float32))


def face_weight(centre, beside):
    return 1.0 + jnp.square(0.5 * (centre + beside))


def fine_stencil(padded, row_valid, down_ok, up_ok):
    centre = padded[1:-1, 1:-1, 1:-1]
    depth = centre.shape[2]
    layers = jnp.arange(depth, dtype=jnp.int32)
    down_z = (layers > 0).astype(jnp.float32)
    up_z = (layers < depth - 1).astype(jnp.float32)
    west = face_weight(centre, padded[:-2, 1:-1, 1:-1])
    east = face_weight(centre, padded[2:, 1:-1, 1:-1])
    south = face_weight(centre, padded[1:-1, :-2, 1:-1])
    north = face_weight(centre, padded[1:-1, 2:, 1:-1])
    below = face_weight(centre, padded[1:-1, 1:-1, :-2])
    above = face_weight(centre, padded[1:-1, 1:-1, 2:])
    diagonal = west + east + south + north + below + above
    rows = row_valid[None, :, None]
    parts = [
        diagonal,
        -west,
        -east,
        -south * down_ok[None, :, None],
        -north * up_ok[None, :, None],
        -below * down_z,
        -above * up_z,
    ]
    return jnp.stack([part * rows for part in parts])


def apply_stencil(stack, offsets, padded):
    size_x, size_y, size_z = stack.shape[1:]
    return sum(
        (
            stack[number]
            * padded[
                1 + offset[0] : 1 + offset[0] + size_x,
                1 + offset[1] : 1 + offset[1] + size_y,
                1 + offset[2] : 1 + offset[2] + size_z,
            ]
            for number, offset in enumerate(offsets)
        )
    )


def galerkin(extended, offsets, row_masks, depth_masks):
    field = jnp.pad(extended, ((0, 0), (0, 0), (0, 0), (1, 0)))
    table = tap_table()
    taps_first = jnp.asarray(np.stack([table[offset[0] + 1] for offset in offsets]))
    taps_second = jnp.asarray(np.stack([table[offset[1] + 1] for offset in offsets]))
    third_stencil_taps = jnp.asarray(np.stack([table[offset[2] + 1] for offset in offsets]))
    depth_in = field.shape[3]
    depth_out = (depth_in - 1) // 2
    fine_index = jnp.arange(depth_in, dtype=jnp.int32)[:, None]
    coarse_index = jnp.arange(depth_out, dtype=jnp.int32)[None, :]
    picker_masks = jnp.stack(
        [(fine_index - 2 * coarse_index == place).astype(jnp.float32) for place in range(3)]
    )
    depth_lookup = jnp.einsum(
        "dql,ljg->djqg", third_stencil_taps, picker_masks, precision=lax.Precision.HIGHEST
    )
    section = jnp.einsum("kxyf,kfsc->ksxyc", field, depth_lookup, precision=lax.Precision.HIGHEST)
    views = strided_views(section, 2)
    section = sum(
        (
            taps_first[:, :, place][:, :, None, None, None, None] * views[place][:, None]
            for place in range(3)
        )
    )
    views = strided_views(section, 4)
    section = sum(
        (
            taps_second[:, :, place][:, None, :, None, None, None, None] * views[place][:, :, None]
            for place in range(3)
        )
    )
    total = jnp.sum(section, 0)
    total = (
        total * row_masks[None, :, None, None, :, None] * depth_masks[None, None, :, None, None, :]
    )
    return total.reshape((27,) + total.shape[3:])


def mask_rows(padded, width):
    inner = padded.shape[1] - 2 * width
    first = lax.axis_index("gy") * inner - width
    rows = first + jnp.arange(padded.shape[1], dtype=jnp.int32)
    total = inner * lax.axis_size("gy")
    keep = ((rows >= 0) & (rows < total)).astype(jnp.float32)
    return padded * keep[None, :, None]


def fine_pad(field):
    padded = with_halo(field, (("gx", 0), ("gy", 1)), 1)
    return jnp.pad(mask_rows(padded, 1), ((0, 0), (0, 0), (1, 1)))


def coarse_pad(field):
    padded = with_halo(field, (("gx", 0), ("gy", 1)), 1)
    return jnp.pad(mask_rows(padded, 1), ((0, 0), (0, 0), (1, 1)))


def lower_extend(stack):
    arrived = from_behind(stack[:, -1:], "gx", 1)
    extended = jnp.concatenate([arrived, stack], 1)
    arrived = shifted(extended[:, :, -1:], "gy", 1)
    return jnp.concatenate([arrived, extended], 2)


def restrict(residual):
    extended = lower_extend(residual[None])[0]
    extended = jnp.pad(extended, ((0, 0), (0, 0), (1, 0)))
    return coarse_sum(coarse_sum(coarse_sum(extended, 0), 1), 2)


def prolong(coarser_grid):
    arrived = from_behind(coarser_grid[:1], "gx", -1)
    finer = alternate(jnp.concatenate([coarser_grid, arrived], 0), 0)
    arrived = shifted(finer[:, :1], "gy", -1)
    finer = alternate(jnp.concatenate([finer, arrived], 1), 1)
    return alternate(jnp.pad(finer, ((0, 0), (0, 0), (0, 1))), 2)


def coarse_solve(stack, source, centre):
    correction = smoothing_weight * source / centre
    for sweep in range(SWEEPS - 1):
        correction = (
            correction
            + smoothing_weight
            * (source - apply_stencil(stack, coarse_offsets, coarse_pad(correction)))
            / centre
        )
    return correction


def cycle(stacks, level, source):
    stack = stacks[level]
    offsets = fine_offsets if level == 0 else coarse_offsets
    centre = stack[offsets.index((0, 0, 0))]
    if level == len(stacks) - 1:
        return coarse_solve(stack, source, centre)
    padder = fine_pad if level == 0 else coarse_pad
    correction = smoothing_weight * source / centre
    residual = source - apply_stencil(stack, offsets, padder(correction))
    correction = correction + prolong(cycle(stacks, level + 1, restrict(residual)))
    return (
        correction
        + smoothing_weight * (source - apply_stencil(stack, offsets, padder(correction))) / centre
    )


def on_device(state, forcing):
    size_x, size_y, size_z = state.shape
    lane = lax.axis_index("gy")
    wide = lax.axis_size("gy")
    total_rows = size_y * wide
    padded = with_halo(state, (("gx", 0), ("gy", 1)), 1)
    padded = jnp.pad(mask_rows(padded, 1), ((0, 0), (0, 0), (1, 1)))
    row_valid, down_ok, up_ok = row_flags(lane * size_y, size_y, total_rows)
    fine = fine_stencil(padded, row_valid, down_ok, up_ok)
    extended = lower_extend(fine)
    newton = forcing - apply_stencil(fine, fine_offsets, padded)
    stacks = [fine]
    offsets = fine_offsets
    for level in range(3):
        coarse_y = (extended.shape[2] - 1) // 2
        coarse_z = extended.shape[3] // 2
        row_masks = edge_masks(lane * coarse_y, coarse_y, coarse_y * wide)
        depth_masks = edge_masks(0, coarse_z, coarse_z)
        coarser_grid = galerkin(extended, offsets, row_masks, depth_masks)
        stacks.append(coarser_grid)
        offsets = coarse_offsets
        if level < 2:
            extended = lower_extend(coarser_grid)
    return state + cycle(stacks, 0, newton)


def solution(mesh):
    placed = (P("gx", "gy", None), P("gx", "gy", None))
    return jax.shard_map(
        on_device, mesh=mesh, in_specs=placed, out_specs=P("gx", "gy", None), check_vma=False
    )
```

profile of v0, /device:TPU:6, one launch (start us, length us, event | category | flops | bytes accessed | tf_op | source)
XLA Modules:
  0.0 396.1 jit_solution(11103454034608487200)
XLA Ops:
  0.7 8.5 %collective-permute-start.1 = (f32[1,16,256]{2,1,0:T(8,128)S(1)}, f32[1,16,256]{2,1,0:T(8,128)S(1)}, u32[]{:S(2)}, u32[]{:S(2)}) collective-permute-start(f32[1,16,256]{2,1,0:T(8,128)S(1)} %get-tuple-element.47), channel_id=1, source_target_pairs={{32,0},{64,32},{96,64},{128,96},{160,128},{192,160},{224,192},{256... | collective-permute-start | bytes 49160 | tf_op jit(solution)/shard_map/ppermute | solution.py:26
  10.1 5.3 %convolution_bitcast_fusion = f32[27,129,3,64,1]{1,0,2,3,4:T(8,128)} fusion(f32[27,3,3,1]{0,2,1,3:T(4,128)} %constant.193, pred[3,129,64,1]{1,2,0,3:T(32,128)(4,1)S(1)} %add_bitcast_fusion.2), kind=kOutput, calls=%fused_computation.7 | convolution fusion | flops 24074496 | bytes 2700684 | tf_op jit(solution)/shard_map/dql,ljg->djqg/dot_general | solution.py:153
  15.4 2.1 convolution_bitcast_fusion.2
  17.5 3.2 convolution_bitcast_fusion.1
  20.9 5.6 %collective-permute-start.3 = (f32[10,1,256]{2,1,0:T(1,128)S(1)}, f32[10,1,256]{2,1,0:T(1,128)S(1)}, u32[]{:S(2)}, u32[]{:S(2)}) collective-permute-start(f32[10,1,256]{2,1,0:T(1,128)S(1)} %get-tuple-element.42), channel_id=1, source_target_pairs={{1,0},{2,1},{3,2},{4,3},{5,4},{6,5},{7,6},{8,7},{9,8},{10,9},{11,1... | collective-permute-start | bytes 30728 | tf_op jit(solution)/shard_map/ppermute | solution.py:26
  28.5 5.7 %collective-permute-done.2 = f32[10,1,256]{2,1,0:T(1,128)S(1)} collective-permute-done((f32[10,1,256]{2,1,0:T(1,128)S(1)}, f32[10,1,256]{2,1,0:T(1,128)S(1)}, u32[]{:S(2)}, u32[]{:S(2)}) %collective-permute-start.2) | collective-permute-done | bytes 10272 | tf_op jit(solution)/shard_map/ppermute | solution.py:23
  36.8 3.0 collective-permute-done.4
  41.7 3.9 collective-permute-start.6
  45.7 3.7 collective-permute-done.6
  49.8 4.3 %collective-permute-done.8 = f32[1,1,16,256]{3,2,1,0:T(8,128)S(1)} collective-permute-done((f32[1,1,16,256]{3,2,1,0:T(8,128)S(1)}, f32[1,1,16,256]{3,2,1,0:T(8,128)S(1)}, u32[]{:S(2)}, u32[]{:S(2)}) %collective-permute-start.8) | collective-permute-done | bytes 16416 | tf_op jit(solution)/shard_map/ppermute | solution.py:34
  57.4 4.4 %collective-permute-done.9 = f32[1,9,1,256]{3,2,1,0:T(1,128)S(1)} collective-permute-done((f32[1,9,1,256]{3,2,1,0:T(1,128)S(1)}, f32[1,9,1,256]{3,2,1,0:T(1,128)S(1)}, u32[]{:S(2)}, u32[]{:S(2)}) %collective-permute-start.9) | collective-permute-done | bytes 9248 | tf_op jit(solution)/shard_map/ppermute | solution.py:40
  62.9 2.1 collective-permute-start.11
  68.6 2.5 collective-permute-done.11
  71.2 7.5 %fusion.29 = f32[7,3,9,17,128]{4,3,2,1,0:T(8,128)S(1)} fusion(f32[7,9,1,256]{3,2,1,0:T(1,128)S(1)} %collective-permute-done.11, f32[7,8,16,256]{3,2,1,0:T(8,128)S(1)} %get-tuple-element.11, f32[7,1,16,256]{3,2,1,0:T(8,128)S(1)} %collective-permute-done.10, f32[7,257,3,128,1]{3,0,2,1,4:T(8,128)} %convolution_bitcast_fusion.1), kind=kOutput, calls=%fused_computation.29 | convolution fusion | flops 1269989632 | bytes 5505024 | tf_op jit(solution)/shard_map/kxyf,kfsc->ksxyc/dot_general | solution.py:156
  80.2 19.3 %slice.1736 = f32[7,3,3,4,8,128]{5,4,3,2,1,0:T(8,128)} slice(f32[7,3,3,4,17,128]{5,4,3,2,1,0:T(8,128)S(1)} %multiply_add_fusion), slice={[0:7:1], [0:3:1], [0:3:1], [0:4:1], [2:17:2], [0:128:1]} | slice | bytes 2064384 | tf_op jit(solution)/shard_map/slice | solution.py:61
  99.5 19.3 %slice.1734 = f32[7,3,3,4,8,128]{5,4,3,2,1,0:T(8,128)} slice(f32[7,3,3,4,17,128]{5,4,3,2,1,0:T(8,128)S(1)} %multiply_add_fusion), slice={[0:7:1], [0:3:1], [0:3:1], [0:4:1], [1:16:2], [0:128:1]} | slice | bytes 2064384 | tf_op jit(solution)/shard_map/slice | solution.py:61
  118.8 19.2 %slice.1732 = f32[7,3,3,4,8,128]{5,4,3,2,1,0:T(8,128)} slice(f32[7,3,3,4,17,128]{5,4,3,2,1,0:T(8,128)S(1)} %multiply_add_fusion), slice={[0:7:1], [0:3:1], [0:3:1], [0:4:1], [0:15:2], [0:128:1]} | slice | bytes 2064384 | tf_op jit(solution)/shard_map/slice | solution.py:59
  138.1 2.7 add_reduce_fusion
  142.4 2.9 collective-permute-done.12
  145.3 3.9 collective-permute-start.15
  151.2 5.6 %collective-permute-done.14 = f32[6,1,128]{2,1,0:T(1,128)S(1)} collective-permute-done((f32[6,1,128]{2,1,0:T(1,128)S(1)}, f32[6,1,128]{2,1,0:T(1,128)S(1)}, u32[]{:S(2)}, u32[]{:S(2)}) %collective-permute-start.14) | collective-permute-done | bytes 3104 | tf_op jit(solution)/shard_map/ppermute | solution.py:23
  157.1 4.2 %collective-permute-done.16 = f32[1,1,8,128]{3,2,1,0:T(8,128)S(1)} collective-permute-done((f32[1,1,8,128]{3,2,1,0:T(8,128)S(1)}, f32[1,1,8,128]{3,2,1,0:T(8,128)S(1)}, u32[]{:S(2)}, u32[]{:S(2)}) %collective-permute-start.16) | collective-permute-done | bytes 4128 | tf_op jit(solution)/shard_map/ppermute | solution.py:34
  163.6 5.3 %collective-permute-done.17 = f32[1,5,1,128]{3,2,1,0:T(1,128)S(1)} collective-permute-done((f32[1,5,1,128]{3,2,1,0:T(1,128)S(1)}, f32[1,5,1,128]{3,2,1,0:T(1,128)S(1)}, u32[]{:S(2)}, u32[]{:S(2)}) %collective-permute-start.17) | collective-permute-done | bytes 2592 | tf_op jit(solution)/shard_map/ppermute | solution.py:40
  169.2 2.1 collective-permute-start.19
  171.8 5.7 %collective-permute-done.19 = f32[27,5,1,128]{3,2,1,0:T(1,128)S(1)} collective-permute-done((f32[27,5,1,128]{3,2,1,0:T(1,128)S(1)}, f32[27,5,1,128]{3,2,1,0:T(1,128)S(1)}, u32[]{:S(2)}, u32[]{:S(2)}) %collective-permute-start.19) | collective-permute-done | bytes 69152 | tf_op jit(solution)/shard_map/ppermute | solution.py:40
  177.5 12.1 %fusion.24 = f32[27,3,5,9,64]{4,3,2,1,0:T(8,128)S(1)} fusion(f32[27,5,1,128]{3,2,1,0:T(1,128)S(1)} %collective-permute-done.19, f32[27,4,8,128]{3,2,1,0:T(8,128)S(1)} %fusion.43, f32[27,1,8,128]{3,2,1,0:T(8,128)S(1)} %collective-permute-done.18, f32[27,129,3,64,1]{1,0,2,3,4:T(8,128)} %convolution_bitcast_fusion), kind=kOutput, calls=%fused_computation.27 | convolution fusion | flops 362057856 | bytes 4230144 | tf_op jit(solution)/shard_map/kxyf,kfsc->ksxyc/dot_general | solution.py:156
  191.3 2.9 multiply_add_fusion.1
  196.3 2.1 add_reduce_fusion.1
  199.8 2.9 collective-permute-done.20
  202.8 3.8 collective-permute-start.23
  208.7 5.5 %collective-permute-done.22 = f32[4,1,64]{2,1,0:T(1,128)S(1)} collective-permute-done((f32[4,1,64]{2,1,0:T(1,128)S(1)}, f32[4,1,64]{2,1,0:T(1,128)S(1)}, u32[]{:S(2)}, u32[]{:S(2)}) %collective-permute-start.22) | collective-permute-done | bytes 1056 | tf_op jit(solution)/shard_map/ppermute | solution.py:23
  214.4 4.2 %collective-permute-done.24 = f32[1,1,4,64]{3,2,1,0:T(4,128)S(1)} collective-permute-done((f32[1,1,4,64]{3,2,1,0:T(4,128)S(1)}, f32[1,1,4,64]{3,2,1,0:T(4,128)S(1)}, u32[]{:S(2)}, u32[]{:S(2)}) %collective-permute-start.24) | collective-permute-done | bytes 1056 | tf_op jit(solution)/shard_map/ppermute | solution.py:34
  221.0 5.2 %collective-permute-done.25 = f32[1,3,1,64]{3,2,1,0:T(1,128)S(1)} collective-permute-done((f32[1,3,1,64]{3,2,1,0:T(1,128)S(1)}, f32[1,3,1,64]{3,2,1,0:T(1,128)S(1)}, u32[]{:S(2)}, u32[]{:S(2)}) %collective-permute-start.25) | collective-permute-done | bytes 800 | tf_op jit(solution)/shard_map/ppermute | solution.py:40
  226.4 2.2 collective-permute-start.27
  229.0 5.4 %collective-permute-done.27 = f32[27,3,1,64]{3,2,1,0:T(1,128)S(1)} collective-permute-done((f32[27,3,1,64]{3,2,1,0:T(1,128)S(1)}, f32[27,3,1,64]{3,2,1,0:T(1,128)S(1)}, u32[]{:S(2)}, u32[]{:S(2)}) %collective-permute-start.27) | collective-permute-done | bytes 20768 | tf_op jit(solution)/shard_map/ppermute | solution.py:40
  234.5 4.8 %convolution_bitcast_fusion.3 = f32[27,3,3,5,32]{4,3,2,1,0:T(8,128)S(1)} fusion(f32[27,65,3,32,1]{1,0,2,3,4:T(8,128)S(1)} %copy-done, f32[27,3,1,64]{3,2,1,0:T(1,128)S(1)} %collective-permute-done.27, f32[27,2,4,64]{3,2,1,0:T(4,128)S(1)} %fusion.87, f32[27,1,4,64]{3,2,1,0:T(4,128)S(1)} %collective-permute-done.26), kind=kOutput, calls=%fused_computation.31 | convolution fusion | flops 30484350 | bytes 933120 | tf_op jit(solution)/shard_map/kxyf,kfsc->ksxyc/dot_general | solution.py:156
  248.0 2.9 collective-permute-done.28
  250.9 3.3 collective-permute-start.31
  254.2 2.5 collective-permute-start.30
  256.8 5.0 %collective-permute-done.30 = f32[3,1,32]{2,1,0:T(1,128)S(1)} collective-permute-done((f32[3,1,32]{2,1,0:T(1,128)S(1)}, f32[3,1,32]{2,1,0:T(1,128)S(1)}, u32[]{:S(2)}, u32[]{:S(2)}) %collective-permute-start.30) | collective-permute-done | bytes 416 | tf_op jit(solution)/shard_map/ppermute | solution.py:23
  263.3 2.9 collective-permute-done.32
  268.2 3.9 collective-permute-start.34
  272.1 3.6 collective-permute-done.34
  277.2 2.9 collective-permute-done.36
  282.1 3.9 collective-permute-start.38
  286.0 3.6 collective-permute-done.38
  291.2 2.9 collective-permute-done.40
  296.0 3.9 collective-permute-start.42
  300.0 3.6 collective-permute-done.42
  305.1 2.9 collective-permute-done.44
  310.0 3.9 collective-permute-start.46
  313.9 3.6 collective-permute-done.46
  321.0 3.5 collective-permute-done.49
  328.0 2.9 collective-permute-done.50
  330.9 4.3 %collective-permute-start.53 = (f32[4,1,64]{2,1,0:T(1,128)S(1)}, f32[4,1,64]{2,1,0:T(1,128)S(1)}, u32[]{:S(2)}, u32[]{:S(2)}) collective-permute-start(f32[4,1,64]{2,1,0:T(1,128)S(1)} %get-tuple-element.58), channel_id=1, source_target_pairs={{1,0},{2,1},{3,2},{4,3},{5,4},{6,5},{7,6},{8,7},{9,8},{10,9},{11,1... | collective-permute-start | bytes 3080 | tf_op jit(solution)/shard_map/ppermute | solution.py:26
  337.1 5.6 %collective-permute-done.52 = f32[4,1,64]{2,1,0:T(1,128)S(1)} collective-permute-done((f32[4,1,64]{2,1,0:T(1,128)S(1)}, f32[4,1,64]{2,1,0:T(1,128)S(1)}, u32[]{:S(2)}, u32[]{:S(2)}) %collective-permute-start.52) | collective-permute-done | bytes 1056 | tf_op jit(solution)/shard_map/ppermute | solution.py:23
  346.3 3.6 collective-permute-done.55
  353.4 2.9 collective-permute-done.56
  356.3 4.3 %collective-permute-start.59 = (f32[6,1,128]{2,1,0:T(1,128)S(1)}, f32[6,1,128]{2,1,0:T(1,128)S(1)}, u32[]{:S(2)}, u32[]{:S(2)}) collective-permute-start(f32[6,1,128]{2,1,0:T(1,128)S(1)} %get-tuple-element.50), channel_id=1, source_target_pairs={{1,0},{2,1},{3,2},{4,3},{5,4},{6,5},{7,6},{8,7},{9,8},{10,9},{11,1... | collective-permute-start | bytes 9224 | tf_op jit(solution)/shard_map/ppermute | solution.py:26
  362.5 5.7 %collective-permute-done.58 = f32[6,1,128]{2,1,0:T(1,128)S(1)} collective-permute-done((f32[6,1,128]{2,1,0:T(1,128)S(1)}, f32[6,1,128]{2,1,0:T(1,128)S(1)}, u32[]{:S(2)}, u32[]{:S(2)}) %collective-permute-start.58) | collective-permute-done | bytes 3104 | tf_op jit(solution)/shard_map/ppermute | solution.py:23
  371.8 3.6 collective-permute-done.61
  379.7 2.9 collective-permute-done.62
  382.7 4.3 %collective-permute-start.65 = (f32[10,1,256]{2,1,0:T(1,128)S(1)}, f32[10,1,256]{2,1,0:T(1,128)S(1)}, u32[]{:S(2)}, u32[]{:S(2)}) collective-permute-start(f32[10,1,256]{2,1,0:T(1,128)S(1)} %get-tuple-element.38), channel_id=1, source_target_pairs={{1,0},{2,1},{3,2},{4,3},{5,4},{6,5},{7,6},{8,7},{9,8},{10,9},{11,1... | collective-permute-start | bytes 30728 | tf_op jit(solution)/shard_map/ppermute | solution.py:26
  388.9 5.7 %collective-permute-done.64 = f32[10,1,256]{2,1,0:T(1,128)S(1)} collective-permute-done((f32[10,1,256]{2,1,0:T(1,128)S(1)}, f32[10,1,256]{2,1,0:T(1,128)S(1)}, u32[]{:S(2)}, u32[]{:S(2)}) %collective-permute-start.64) | collective-permute-done | bytes 10272 | tf_op jit(solution)/shard_map/ppermute | solution.py:23
  (376 shorter events, 85.2 us)
Async XLA Ops:
  0.7 20.0 %collective-permute-start = (f32[1,16,256]{2,1,0:T(8,128)S(1)}, f32[1,16,256]{2,1,0:T(8,128)S(1)}, u32[]{:S(2)}, u32[]{:S(2)}) collective-permute-start(f32[1,16,256]{2,1,0:T(8,128)S(1)} %get-tuple-element.48), channel_id=1, source_target_pairs={{0,32},{32,64},{64,96},{96,128},{128,160},{160,192},{192,224},{224... | collective-permute-start | bytes 49160 | tf_op jit(solution)/shard_map/ppermute | solution.py:23
  0.7 20.1 %collective-permute-start.1 = (f32[1,16,256]{2,1,0:T(8,128)S(1)}, f32[1,16,256]{2,1,0:T(8,128)S(1)}, u32[]{:S(2)}, u32[]{:S(2)}) collective-permute-start(f32[1,16,256]{2,1,0:T(8,128)S(1)} %get-tuple-element.47), channel_id=1, source_target_pairs={{32,0},{64,32},{96,64},{128,96},{160,128},{192,160},{224,192},{256... | collective-permute-start | bytes 49160 | tf_op jit(solution)/shard_map/ppermute | solution.py:26
  20.9 7.6 %collective-permute-start.3 = (f32[10,1,256]{2,1,0:T(1,128)S(1)}, f32[10,1,256]{2,1,0:T(1,128)S(1)}, u32[]{:S(2)}, u32[]{:S(2)}) collective-permute-start(f32[10,1,256]{2,1,0:T(1,128)S(1)} %get-tuple-element.42), channel_id=1, source_target_pairs={{1,0},{2,1},{3,2},{4,3},{5,4},{6,5},{7,6},{8,7},{9,8},{10,9},{11,1... | collective-permute-start | bytes 30728 | tf_op jit(solution)/shard_map/ppermute | solution.py:26
  26.5 7.7 %collective-permute-start.2 = (f32[10,1,256]{2,1,0:T(1,128)S(1)}, f32[10,1,256]{2,1,0:T(1,128)S(1)}, u32[]{:S(2)}, u32[]{:S(2)}) collective-permute-start(f32[10,1,256]{2,1,0:T(1,128)S(1)} %get-tuple-element.41), channel_id=1, source_target_pairs={{0,1},{1,2},{2,3},{3,4},{4,5},{5,6},{6,7},{7,8},{8,9},{9,10},{10,1... | collective-permute-start | bytes 30728 | tf_op jit(solution)/shard_map/ppermute | solution.py:23
  35.3 1.5 collective-permute-start.5
  35.4 4.4 %collective-permute-start.4 = (f32[1,16,256]{2,1,0:T(8,128)S(1)}, f32[1,16,256]{2,1,0:T(8,128)S(1)}, u32[]{:S(2)}, u32[]{:S(2)}) collective-permute-start(f32[1,16,256]{2,1,0:T(8,128)S(1)} %get-tuple-element.45), channel_id=1, source_target_pairs={{0,32},{32,64},{64,96},{96,128},{128,160},{160,192},{192,224},{224... | collective-permute-start | bytes 49160 | tf_op jit(solution)/shard_map/ppermute | solution.py:23
  39.8 5.9 %collective-permute-start.7 = (f32[10,1,256]{2,1,0:T(1,128)S(1)}, f32[10,1,256]{2,1,0:T(1,128)S(1)}, u32[]{:S(2)}, u32[]{:S(2)}) collective-permute-start(f32[10,1,256]{2,1,0:T(1,128)S(1)} %get-tuple-element.40), channel_id=1, source_target_pairs={{1,0},{2,1},{3,2},{4,3},{5,4},{6,5},{7,6},{8,7},{9,8},{10,9},{11,1... | collective-permute-start | bytes 30728 | tf_op jit(solution)/shard_map/ppermute | solution.py:26
  41.7 7.7 %collective-permute-start.6 = (f32[10,1,256]{2,1,0:T(1,128)S(1)}, f32[10,1,256]{2,1,0:T(1,128)S(1)}, u32[]{:S(2)}, u32[]{:S(2)}) collective-permute-start(f32[10,1,256]{2,1,0:T(1,128)S(1)} %get-tuple-element.39), channel_id=1, source_target_pairs={{0,1},{1,2},{2,3},{3,4},{4,5},{5,6},{6,7},{7,8},{8,9},{9,10},{10,1... | collective-permute-start | bytes 30728 | tf_op jit(solution)/shard_map/ppermute | solution.py:23
  49.7 4.4 %collective-permute-start.8 = (f32[1,1,16,256]{3,2,1,0:T(8,128)S(1)}, f32[1,1,16,256]{3,2,1,0:T(8,128)S(1)}, u32[]{:S(2)}, u32[]{:S(2)}) collective-permute-start(f32[1,1,16,256]{3,2,1,0:T(8,128)S(1)} %slice.2175), channel_id=1, source_target_pairs={{0,32},{32,64},{64,96},{96,128},{128,160},{160,192},{192,224},{224... | collective-permute-start | bytes 49160 | tf_op jit(solution)/shard_map/ppermute | solution.py:34
  54.1 7.7 %collective-permute-start.9 = (f32[1,9,1,256]{3,2,1,0:T(1,128)S(1)}, f32[1,9,1,256]{3,2,1,0:T(1,128)S(1)}, u32[]{:S(2)}, u32[]{:S(2)}) collective-permute-start(f32[1,9,1,256]{3,2,1,0:T(1,128)S(1)} %pad_maximum_fusion.16), channel_id=1, source_target_pairs={{0,1},{1,2},{2,3},{3,4},{4,5},{5,6},{6,7},{7,8},{8,9},{9,10},{10,1... | collective-permute-start | bytes 27656 | tf_op jit(solution)/shard_map/ppermute | solution.py:40
  57.4 5.4 %collective-permute-start.10 = (f32[7,1,16,256]{3,2,1,0:T(8,128)S(1)}, f32[7,1,16,256]{3,2,1,0:T(8,128)S(1)}, u32[]{:S(2)}, u32[]{:S(2)}) collective-permute-start(f32[7,1,16,256]{3,2,1,0:T(8,128)S(1)} %slice.2176), channel_id=1, source_target_pairs={{0,32},{32,64},{64,96},{96,128},{128,160},{160,192},{192,224},{224... | collective-permute-start | bytes 344072 | tf_op jit(solution)/shard_map/ppermute | solution.py:34
  62.9 8.3 %collective-permute-start.11 = (f32[7,9,1,256]{3,2,1,0:T(1,128)S(1)}, f32[7,9,1,256]{3,2,1,0:T(1,128)S(1)}, u32[]{:S(2)}, u32[]{:S(2)}) collective-permute-start(f32[7,9,1,256]{3,2,1,0:T(1,128)S(1)} %pad_maximum_fusion.3), channel_id=1, source_target_pairs={{0,1},{1,2},{2,3},{3,4},{4,5},{5,6},{6,7},{7,8},{8,9},{9,10},{10,1... | collective-permute-start | bytes 193544 | tf_op jit(solution)/shard_map/ppermute | solution.py:40
  141.0 1.3 collective-permute-start.13
  141.0 4.3 %collective-permute-start.12 = (f32[1,8,128]{2,1,0:T(8,128)S(1)}, f32[1,8,128]{2,1,0:T(8,128)S(1)}, u32[]{:S(2)}, u32[]{:S(2)}) collective-permute-start(f32[1,8,128]{2,1,0:T(8,128)S(1)} %get-tuple-element.55), channel_id=1, source_target_pairs={{0,32},{32,64},{64,96},{96,128},{128,160},{160,192},{192,224},{224... | collective-permute-start | bytes 12296 | tf_op jit(solution)/shard_map/ppermute | solution.py:23
  145.3 5.9 %collective-permute-start.15 = (f32[6,1,128]{2,1,0:T(1,128)S(1)}, f32[6,1,128]{2,1,0:T(1,128)S(1)}, u32[]{:S(2)}, u32[]{:S(2)}) collective-permute-start(f32[6,1,128]{2,1,0:T(1,128)S(1)} %get-tuple-element.52), channel_id=1, source_target_pairs={{1,0},{2,1},{3,2},{4,3},{5,4},{6,5},{7,6},{8,7},{9,8},{10,9},{11,1... | collective-permute-start | bytes 9224 | tf_op jit(solution)/shard_map/ppermute | solution.py:26
  149.2 7.6 %collective-permute-start.14 = (f32[6,1,128]{2,1,0:T(1,128)S(1)}, f32[6,1,128]{2,1,0:T(1,128)S(1)}, u32[]{:S(2)}, u32[]{:S(2)}) collective-permute-start(f32[6,1,128]{2,1,0:T(1,128)S(1)} %get-tuple-element.51), channel_id=1, source_target_pairs={{0,1},{1,2},{2,3},{3,4},{4,5},{5,6},{6,7},{7,8},{8,9},{9,10},{10,1... | collective-permute-start | bytes 9224 | tf_op jit(solution)/shard_map/ppermute | solution.py:23
  157.1 4.3 %collective-permute-start.16 = (f32[1,1,8,128]{3,2,1,0:T(8,128)S(1)}, f32[1,1,8,128]{3,2,1,0:T(8,128)S(1)}, u32[]{:S(2)}, u32[]{:S(2)}) collective-permute-start(f32[1,1,8,128]{3,2,1,0:T(8,128)S(1)} %slice.2215), channel_id=1, source_target_pairs={{0,32},{32,64},{64,96},{96,128},{128,160},{160,192},{192,224},{224... | collective-permute-start | bytes 12296 | tf_op jit(solution)/shard_map/ppermute | solution.py:34
  161.3 7.6 %collective-permute-start.17 = (f32[1,5,1,128]{3,2,1,0:T(1,128)S(1)}, f32[1,5,1,128]{3,2,1,0:T(1,128)S(1)}, u32[]{:S(2)}, u32[]{:S(2)}) collective-permute-start(f32[1,5,1,128]{3,2,1,0:T(1,128)S(1)} %pad_maximum_fusion.33), channel_id=1, source_target_pairs={{0,1},{1,2},{2,3},{3,4},{4,5},{5,6},{6,7},{7,8},{8,9},{9,10},{10,1... | collective-permute-start | bytes 7688 | tf_op jit(solution)/shard_map/ppermute | solution.py:40
  163.6 5.5 %collective-permute-start.18 = (f32[27,1,8,128]{3,2,1,0:T(8,128)S(1)}, f32[27,1,8,128]{3,2,1,0:T(8,128)S(1)}, u32[]{:S(2)}, u32[]{:S(2)}) collective-permute-start(f32[27,1,8,128]{3,2,1,0:T(8,128)S(1)} %slice.2216), channel_id=1, source_target_pairs={{0,32},{32,64},{64,96},{96,128},{128,160},{160,192},{192,224},{224... | collective-permute-start | bytes 331784 | tf_op jit(solution)/shard_map/ppermute | solution.py:34
  169.2 8.3 %collective-permute-start.19 = (f32[27,5,1,128]{3,2,1,0:T(1,128)S(1)}, f32[27,5,1,128]{3,2,1,0:T(1,128)S(1)}, u32[]{:S(2)}, u32[]{:S(2)}) collective-permute-start(f32[27,5,1,128]{3,2,1,0:T(1,128)S(1)} %pad_maximum_fusion.1), channel_id=1, source_target_pairs={{0,1},{1,2},{2,3},{3,4},{4,5},{5,6},{6,7},{7,8},{8,9},{9,10},{10,1... | collective-permute-start | bytes 207368 | tf_op jit(solution)/shard_map/ppermute | solution.py:40
  198.5 1.3 collective-permute-start.21
  198.5 4.2 %collective-permute-start.20 = (f32[1,4,64]{2,1,0:T(4,128)S(1)}, f32[1,4,64]{2,1,0:T(4,128)S(1)}, u32[]{:S(2)}, u32[]{:S(2)}) collective-permute-start(f32[1,4,64]{2,1,0:T(4,128)S(1)} %get-tuple-element.63), channel_id=1, source_target_pairs={{0,32},{32,64},{64,96},{96,128},{128,160},{160,192},{192,224},{224... | collective-permute-start | bytes 3080 | tf_op jit(solution)/shard_map/ppermute | solution.py:23
  202.8 5.9 %collective-permute-start.23 = (f32[4,1,64]{2,1,0:T(1,128)S(1)}, f32[4,1,64]{2,1,0:T(1,128)S(1)}, u32[]{:S(2)}, u32[]{:S(2)}) collective-permute-start(f32[4,1,64]{2,1,0:T(1,128)S(1)} %get-tuple-element.60), channel_id=1, source_target_pairs={{1,0},{2,1},{3,2},{4,3},{5,4},{6,5},{7,6},{8,7},{9,8},{10,9},{11,1... | collective-permute-start | bytes 3080 | tf_op jit(solution)/shard_map/ppermute | solution.py:26
  206.6 7.6 %collective-permute-start.22 = (f32[4,1,64]{2,1,0:T(1,128)S(1)}, f32[4,1,64]{2,1,0:T(1,128)S(1)}, u32[]{:S(2)}, u32[]{:S(2)}) collective-permute-start(f32[4,1,64]{2,1,0:T(1,128)S(1)} %get-tuple-element.59), channel_id=1, source_target_pairs={{0,1},{1,2},{2,3},{3,4},{4,5},{5,6},{6,7},{7,8},{8,9},{9,10},{10,1... | collective-permute-start | bytes 3080 | tf_op jit(solution)/shard_map/ppermute | solution.py:23
  214.4 4.2 %collective-permute-start.24 = (f32[1,1,4,64]{3,2,1,0:T(4,128)S(1)}, f32[1,1,4,64]{3,2,1,0:T(4,128)S(1)}, u32[]{:S(2)}, u32[]{:S(2)}) collective-permute-start(f32[1,1,4,64]{3,2,1,0:T(4,128)S(1)} %slice.2255), channel_id=1, source_target_pairs={{0,32},{32,64},{64,96},{96,128},{128,160},{160,192},{192,224},{224... | collective-permute-start | bytes 3080 | tf_op jit(solution)/shard_map/ppermute | solution.py:34
  218.7 7.6 %collective-permute-start.25 = (f32[1,3,1,64]{3,2,1,0:T(1,128)S(1)}, f32[1,3,1,64]{3,2,1,0:T(1,128)S(1)}, u32[]{:S(2)}, u32[]{:S(2)}) collective-permute-start(f32[1,3,1,64]{3,2,1,0:T(1,128)S(1)} %pad_maximum_fusion.42), channel_id=1, source_target_pairs={{0,1},{1,2},{2,3},{3,4},{4,5},{5,6},{6,7},{7,8},{8,9},{9,10},{10,1... | collective-permute-start | bytes 2312 | tf_op jit(solution)/shard_map/ppermute | solution.py:40
  220.9 5.4 %collective-permute-start.26 = (f32[27,1,4,64]{3,2,1,0:T(4,128)S(1)}, f32[27,1,4,64]{3,2,1,0:T(4,128)S(1)}, u32[]{:S(2)}, u32[]{:S(2)}) collective-permute-start(f32[27,1,4,64]{3,2,1,0:T(4,128)S(1)} %slice.2256), channel_id=1, source_target_pairs={{0,32},{32,64},{64,96},{96,128},{128,160},{160,192},{192,224},{224... | collective-permute-start | bytes 82952 | tf_op jit(solution)/shard_map/ppermute | solution.py:34
  226.4 8.0 %collective-permute-start.27 = (f32[27,3,1,64]{3,2,1,0:T(1,128)S(1)}, f32[27,3,1,64]{3,2,1,0:T(1,128)S(1)}, u32[]{:S(2)}, u32[]{:S(2)}) collective-permute-start(f32[27,3,1,64]{3,2,1,0:T(1,128)S(1)} %pad_maximum_fusion.4), channel_id=1, source_target_pairs={{0,1},{1,2},{2,3},{3,4},{4,5},{5,6},{6,7},{7,8},{8,9},{9,10},{10,1... | collective-permute-start | bytes 62216 | tf_op jit(solution)/shard_map/ppermute | solution.py:40
  246.7 1.3 collective-permute-start.29
  246.7 4.2 %collective-permute-start.28 = (f32[1,2,32]{2,1,0:T(2,128)S(1)}, f32[1,2,32]{2,1,0:T(2,128)S(1)}, u32[]{:S(2)}, u32[]{:S(2)}) collective-permute-start(f32[1,2,32]{2,1,0:T(2,128)S(1)} %get-tuple-element.5), channel_id=1, source_target_pairs={{0,32},{32,64},{64,96},{96,128},{128,160},{160,192},{192,224},{224... | collective-permute-start | bytes 776 | tf_op jit(solution)/shard_map/ppermute | solution.py:23
  250.9 5.9 %collective-permute-start.31 = (f32[3,1,32]{2,1,0:T(1,128)S(1)}, f32[3,1,32]{2,1,0:T(1,128)S(1)}, u32[]{:S(2)}, u32[]{:S(2)}) collective-permute-start(f32[3,1,32]{2,1,0:T(1,128)S(1)} %get-tuple-element.74), channel_id=1, source_target_pairs={{1,0},{2,1},{3,2},{4,3},{5,4},{6,5},{7,6},{8,7},{9,8},{10,9},{11,1... | collective-permute-start | bytes 1160 | tf_op jit(solution)/shard_map/ppermute | solution.py:26
  254.2 7.6 %collective-permute-start.30 = (f32[3,1,32]{2,1,0:T(1,128)S(1)}, f32[3,1,32]{2,1,0:T(1,128)S(1)}, u32[]{:S(2)}, u32[]{:S(2)}) collective-permute-start(f32[3,1,32]{2,1,0:T(1,128)S(1)} %get-tuple-element.73), channel_id=1, source_target_pairs={{0,1},{1,2},{2,3},{3,4},{4,5},{5,6},{6,7},{7,8},{8,9},{9,10},{10,1... | collective-permute-start | bytes 1160 | tf_op jit(solution)/shard_map/ppermute | solution.py:23
  262.0 1.3 collective-permute-start.33
  262.0 4.2 %collective-permute-start.32 = (f32[1,2,32]{2,1,0:T(2,128)S(1)}, f32[1,2,32]{2,1,0:T(2,128)S(1)}, u32[]{:S(2)}, u32[]{:S(2)}) collective-permute-start(f32[1,2,32]{2,1,0:T(2,128)S(1)} %divide_add_fusion.4), channel_id=1, source_target_pairs={{0,32},{32,64},{64,96},{96,128},{128,160},{160,192},{192,224},{224... | collective-permute-start | bytes 776 | tf_op jit(solution)/shard_map/ppermute | solution.py:23
  266.2 5.9 %collective-permute-start.35 = (f32[3,1,32]{2,1,0:T(1,128)S(1)}, f32[3,1,32]{2,1,0:T(1,128)S(1)}, u32[]{:S(2)}, u32[]{:S(2)}) collective-permute-start(f32[3,1,32]{2,1,0:T(1,128)S(1)} %get-tuple-element.72), channel_id=1, source_target_pairs={{1,0},{2,1},{3,2},{4,3},{5,4},{6,5},{7,6},{8,7},{9,8},{10,9},{11,1... | collective-permute-start | bytes 1160 | tf_op jit(solution)/shard_map/ppermute | solution.py:26
  268.2 7.6 %collective-permute-start.34 = (f32[3,1,32]{2,1,0:T(1,128)S(1)}, f32[3,1,32]{2,1,0:T(1,128)S(1)}, u32[]{:S(2)}, u32[]{:S(2)}) collective-permute-start(f32[3,1,32]{2,1,0:T(1,128)S(1)} %get-tuple-element.71), channel_id=1, source_target_pairs={{0,1},{1,2},{2,3},{3,4},{4,5},{5,6},{6,7},{7,8},{8,9},{9,10},{10,1... | collective-permute-start | bytes 1160 | tf_op jit(solution)/shard_map/ppermute | solution.py:23
  275.9 1.3 collective-permute-start.37
  275.9 4.2 %collective-permute-start.36 = (f32[1,2,32]{2,1,0:T(2,128)S(1)}, f32[1,2,32]{2,1,0:T(2,128)S(1)}, u32[]{:S(2)}, u32[]{:S(2)}) collective-permute-start(f32[1,2,32]{2,1,0:T(2,128)S(1)} %divide_add_fusion.3), channel_id=1, source_target_pairs={{0,32},{32,64},{64,96},{96,128},{128,160},{160,192},{192,224},{224... | collective-permute-start | bytes 776 | tf_op jit(solution)/shard_map/ppermute | solution.py:23
  280.2 5.9 %collective-permute-start.39 = (f32[3,1,32]{2,1,0:T(1,128)S(1)}, f32[3,1,32]{2,1,0:T(1,128)S(1)}, u32[]{:S(2)}, u32[]{:S(2)}) collective-permute-start(f32[3,1,32]{2,1,0:T(1,128)S(1)} %get-tuple-element.70), channel_id=1, source_target_pairs={{1,0},{2,1},{3,2},{4,3},{5,4},{6,5},{7,6},{8,7},{9,8},{10,9},{11,1... | collective-permute-start | bytes 1160 | tf_op jit(solution)/shard_map/ppermute | solution.py:26
  282.1 7.6 %collective-permute-start.38 = (f32[3,1,32]{2,1,0:T(1,128)S(1)}, f32[3,1,32]{2,1,0:T(1,128)S(1)}, u32[]{:S(2)}, u32[]{:S(2)}) collective-permute-start(f32[3,1,32]{2,1,0:T(1,128)S(1)} %get-tuple-element.69), channel_id=1, source_target_pairs={{0,1},{1,2},{2,3},{3,4},{4,5},{5,6},{6,7},{7,8},{8,9},{9,10},{10,1... | collective-permute-start | bytes 1160 | tf_op jit(solution)/shard_map/ppermute | solution.py:23
  289.9 1.3 collective-permute-start.41
  289.9 4.2 %collective-permute-start.40 = (f32[1,2,32]{2,1,0:T(2,128)S(1)}, f32[1,2,32]{2,1,0:T(2,128)S(1)}, u32[]{:S(2)}, u32[]{:S(2)}) collective-permute-start(f32[1,2,32]{2,1,0:T(2,128)S(1)} %divide_add_fusion.2), channel_id=1, source_target_pairs={{0,32},{32,64},{64,96},{96,128},{128,160},{160,192},{192,224},{224... | collective-permute-start | bytes 776 | tf_op jit(solution)/shard_map/ppermute | solution.py:23
  294.1 5.9 %collective-permute-start.43 = (f32[3,1,32]{2,1,0:T(1,128)S(1)}, f32[3,1,32]{2,1,0:T(1,128)S(1)}, u32[]{:S(2)}, u32[]{:S(2)}) collective-permute-start(f32[3,1,32]{2,1,0:T(1,128)S(1)} %get-tuple-element.68), channel_id=1, source_target_pairs={{1,0},{2,1},{3,2},{4,3},{5,4},{6,5},{7,6},{8,7},{9,8},{10,9},{11,1... | collective-permute-start | bytes 1160 | tf_op jit(solution)/shard_map/ppermute | solution.py:26
  296.0 7.6 %collective-permute-start.42 = (f32[3,1,32]{2,1,0:T(1,128)S(1)}, f32[3,1,32]{2,1,0:T(1,128)S(1)}, u32[]{:S(2)}, u32[]{:S(2)}) collective-permute-start(f32[3,1,32]{2,1,0:T(1,128)S(1)} %get-tuple-element.67), channel_id=1, source_target_pairs={{0,1},{1,2},{2,3},{3,4},{4,5},{5,6},{6,7},{7,8},{8,9},{9,10},{10,1... | collective-permute-start | bytes 1160 | tf_op jit(solution)/shard_map/ppermute | solution.py:23
  303.8 4.2 %collective-permute-start.44 = (f32[1,2,32]{2,1,0:T(2,128)S(1)}, f32[1,2,32]{2,1,0:T(2,128)S(1)}, u32[]{:S(2)}, u32[]{:S(2)}) collective-permute-start(f32[1,2,32]{2,1,0:T(2,128)S(1)} %divide_add_fusion.1), channel_id=1, source_target_pairs={{0,32},{32,64},{64,96},{96,128},{128,160},{160,192},{192,224},{224... | collective-permute-start | bytes 776 | tf_op jit(solution)/shard_map/ppermute | solution.py:23
  308.1 5.9 %collective-permute-start.47 = (f32[3,1,32]{2,1,0:T(1,128)S(1)}, f32[3,1,32]{2,1,0:T(1,128)S(1)}, u32[]{:S(2)}, u32[]{:S(2)}) collective-permute-start(f32[3,1,32]{2,1,0:T(1,128)S(1)} %get-tuple-element.66), channel_id=1, source_target_pairs={{1,0},{2,1},{3,2},{4,3},{5,4},{6,5},{7,6},{8,7},{9,8},{10,9},{11,1... | collective-permute-start | bytes 1160 | tf_op jit(solution)/shard_map/ppermute | solution.py:26
  310.0 7.6 %collective-permute-start.46 = (f32[3,1,32]{2,1,0:T(1,128)S(1)}, f32[3,1,32]{2,1,0:T(1,128)S(1)}, u32[]{:S(2)}, u32[]{:S(2)}) collective-permute-start(f32[3,1,32]{2,1,0:T(1,128)S(1)} %get-tuple-element.65), channel_id=1, source_target_pairs={{0,1},{1,2},{2,3},{3,4},{4,5},{5,6},{6,7},{7,8},{8,9},{9,10},{10,1... | collective-permute-start | bytes 1160 | tf_op jit(solution)/shard_map/ppermute | solution.py:23
  319.1 5.5 %collective-permute-start.49 = (f32[2,1,32]{2,1,0:T(1,128)S(1)}, f32[2,1,32]{2,1,0:T(1,128)S(1)}, u32[]{:S(2)}, u32[]{:S(2)}) collective-permute-start(f32[2,1,32]{2,1,0:T(1,128)S(1)} %slice.2342), channel_id=1, source_target_pairs={{1,0},{2,1},{3,2},{4,3},{5,4},{6,5},{7,6},{8,7},{9,8},{10,9},{11,1... | collective-permute-start | bytes 776 | tf_op jit(solution)/shard_map/ppermute | solution.py:40
  324.9 3.1 collective-permute-start.51
  326.7 4.2 %collective-permute-start.50 = (f32[1,4,64]{2,1,0:T(4,128)S(1)}, f32[1,4,64]{2,1,0:T(4,128)S(1)}, u32[]{:S(2)}, u32[]{:S(2)}) collective-permute-start(f32[1,4,64]{2,1,0:T(4,128)S(1)} %get-tuple-element.61), channel_id=1, source_target_pairs={{0,32},{32,64},{64,96},{96,128},{128,160},{160,192},{192,224},{224... | collective-permute-start | bytes 3080 | tf_op jit(solution)/shard_map/ppermute | solution.py:23
  330.9 6.2 %collective-permute-start.53 = (f32[4,1,64]{2,1,0:T(1,128)S(1)}, f32[4,1,64]{2,1,0:T(1,128)S(1)}, u32[]{:S(2)}, u32[]{:S(2)}) collective-permute-start(f32[4,1,64]{2,1,0:T(1,128)S(1)} %get-tuple-element.58), channel_id=1, source_target_pairs={{1,0},{2,1},{3,2},{4,3},{5,4},{6,5},{7,6},{8,7},{9,8},{10,9},{11,1... | collective-permute-start | bytes 3080 | tf_op jit(solution)/shard_map/ppermute | solution.py:26
  335.2 7.6 %collective-permute-start.52 = (f32[4,1,64]{2,1,0:T(1,128)S(1)}, f32[4,1,64]{2,1,0:T(1,128)S(1)}, u32[]{:S(2)}, u32[]{:S(2)}) collective-permute-start(f32[4,1,64]{2,1,0:T(1,128)S(1)} %get-tuple-element.57), channel_id=1, source_target_pairs={{0,1},{1,2},{2,3},{3,4},{4,5},{5,6},{6,7},{7,8},{8,9},{9,10},{10,1... | collective-permute-start | bytes 3080 | tf_op jit(solution)/shard_map/ppermute | solution.py:23
  343.0 1.3 collective-permute-start.54
  344.4 5.5 %collective-permute-start.55 = (f32[4,1,64]{2,1,0:T(1,128)S(1)}, f32[4,1,64]{2,1,0:T(1,128)S(1)}, u32[]{:S(2)}, u32[]{:S(2)}) collective-permute-start(f32[4,1,64]{2,1,0:T(1,128)S(1)} %slice.2355), channel_id=1, source_target_pairs={{1,0},{2,1},{3,2},{4,3},{5,4},{6,5},{7,6},{8,7},{9,8},{10,9},{11,1... | collective-permute-start | bytes 3080 | tf_op jit(solution)/shard_map/ppermute | solution.py:40
  350.3 3.1 collective-permute-start.57
  352.0 4.2 %collective-permute-start.56 = (f32[1,8,128]{2,1,0:T(8,128)S(1)}, f32[1,8,128]{2,1,0:T(8,128)S(1)}, u32[]{:S(2)}, u32[]{:S(2)}) collective-permute-start(f32[1,8,128]{2,1,0:T(8,128)S(1)} %get-tuple-element.53), channel_id=1, source_target_pairs={{0,32},{32,64},{64,96},{96,128},{128,160},{160,192},{192,224},{224... | collective-permute-start | bytes 12296 | tf_op jit(solution)/shard_map/ppermute | solution.py:23
  356.3 6.2 %collective-permute-start.59 = (f32[6,1,128]{2,1,0:T(1,128)S(1)}, f32[6,1,128]{2,1,0:T(1,128)S(1)}, u32[]{:S(2)}, u32[]{:S(2)}) collective-permute-start(f32[6,1,128]{2,1,0:T(1,128)S(1)} %get-tuple-element.50), channel_id=1, source_target_pairs={{1,0},{2,1},{3,2},{4,3},{5,4},{6,5},{7,6},{8,7},{9,8},{10,9},{11,1... | collective-permute-start | bytes 9224 | tf_op jit(solution)/shard_map/ppermute | solution.py:26
  360.6 7.6 %collective-permute-start.58 = (f32[6,1,128]{2,1,0:T(1,128)S(1)}, f32[6,1,128]{2,1,0:T(1,128)S(1)}, u32[]{:S(2)}, u32[]{:S(2)}) collective-permute-start(f32[6,1,128]{2,1,0:T(1,128)S(1)} %get-tuple-element.49), channel_id=1, source_target_pairs={{0,1},{1,2},{2,3},{3,4},{4,5},{5,6},{6,7},{7,8},{8,9},{9,10},{10,1... | collective-permute-start | bytes 9224 | tf_op jit(solution)/shard_map/ppermute | solution.py:23
  368.5 1.3 collective-permute-start.60
  369.9 5.5 %collective-permute-start.61 = (f32[8,1,128]{2,1,0:T(1,128)S(1)}, f32[8,1,128]{2,1,0:T(1,128)S(1)}, u32[]{:S(2)}, u32[]{:S(2)}) collective-permute-start(f32[8,1,128]{2,1,0:T(1,128)S(1)} %slice.2368), channel_id=1, source_target_pairs={{1,0},{2,1},{3,2},{4,3},{5,4},{6,5},{7,6},{8,7},{9,8},{10,9},{11,1... | collective-permute-start | bytes 12296 | tf_op jit(solution)/shard_map/ppermute | solution.py:40
  376.5 3.2 collective-permute-start.63
  378.3 4.4 %collective-permute-start.62 = (f32[1,16,256]{2,1,0:T(8,128)S(1)}, f32[1,16,256]{2,1,0:T(8,128)S(1)}, u32[]{:S(2)}, u32[]{:S(2)}) collective-permute-start(f32[1,16,256]{2,1,0:T(8,128)S(1)} %get-tuple-element.43), channel_id=1, source_target_pairs={{0,32},{32,64},{64,96},{96,128},{128,160},{160,192},{192,224},{224... | collective-permute-start | bytes 49160 | tf_op jit(solution)/shard_map/ppermute | solution.py:23
  382.7 6.2 %collective-permute-start.65 = (f32[10,1,256]{2,1,0:T(1,128)S(1)}, f32[10,1,256]{2,1,0:T(1,128)S(1)}, u32[]{:S(2)}, u32[]{:S(2)}) collective-permute-start(f32[10,1,256]{2,1,0:T(1,128)S(1)} %get-tuple-element.38), channel_id=1, source_target_pairs={{1,0},{2,1},{3,2},{4,3},{5,4},{6,5},{7,6},{8,7},{9,8},{10,9},{11,1... | collective-permute-start | bytes 30728 | tf_op jit(solution)/shard_map/ppermute | solution.py:26
  387.0 7.7 %collective-permute-start.64 = (f32[10,1,256]{2,1,0:T(1,128)S(1)}, f32[10,1,256]{2,1,0:T(1,128)S(1)}, u32[]{:S(2)}, u32[]{:S(2)}) collective-permute-start(f32[10,1,256]{2,1,0:T(1,128)S(1)} %get-tuple-element.37), channel_id=1, source_target_pairs={{0,1},{1,2},{2,3},{3,4},{4,5},{5,6},{6,7},{7,8},{8,9},{9,10},{10,1... | collective-permute-start | bytes 30728 | tf_op jit(solution)/shard_map/ppermute | solution.py:23
  (48 other events, 786.9 us)
where the time goes:
time: 403 us; the launch traced here: 396 us
  waiting for transfers between devices  156 us (39%)
  starting transfers between devices  109 us (27%)
  local copies, waits for them, and re-layouts  76.2 us (19%)
  matrix products  35 us (9%)
  other arithmetic  17.5 us (4%)
    ppermute x24, waiting for transfers between devices, with_halo(): lax.ppermute(lax.slice_in_dim(block, block.shape[dim] - width, None, axis...  89.4 us
    ppermute x24, starting transfers between devices, with_halo(): lax.ppermute(lax.slice_in_dim(block, 0, width, axis=dim), axis, backward)  53.1 us
    slice x20, local copies, waits for them, and re-layouts, strided_views(): lax.slice_in_dim(field, start, count + 1 if start == 2 else count, 2, axis)  46.8 us
    ppermute x9, waiting for transfers between devices, shifted(): return lax.ppermute(value, axis, pairs)  39.2 us
    ppermute x24, starting transfers between devices, with_halo(): lax.ppermute(lax.slice_in_dim(block, block.shape[dim] - width, None, axis...  37.8 us
    slice x13, local copies, waits for them, and re-layouts, strided_views(): lax.slice_in_dim(field, start, start + count - 1, 2, axis)  25.1 us
    dot_general x3, matrix products, galerkin(): jnp.einsum('kxyf,kfsc->ksxyc', field, depth_lookup, precision=lax.Precisi...  24.3 us
    ppermute x9, starting transfers between devices, shifted(): return lax.ppermute(value, axis, pairs)  17.9 us
  transfers between devices with their start and end apart: 66, of which 50 were waited for; matrix products, arithmetic and copies ran while one was open for 5% of the time, Pallas kernels for 0%

commit v1 on v0

v1 whole, which is shorter than its diff:
```python
import jax
import jax.numpy as jnp
from jax import lax
from jax.experimental import pallas as pl
from jax.experimental.pallas import tpu as pltpu
from jax.sharding import PartitionSpec as P

WEIGHT = 0.6
MESH = pl.DeviceIdType.MESH
F32 = jnp.float32

AROUND = [(a, b) for a in (-1, 0, 1) for b in (-1, 0, 1) if (a, b) != (0, 0)]
WIDE = [(a, b) for a in range(-3, 5) for b in range(-2, 3) if (a, b) != (0, 0)]
GREETED = [(a, b) for a in range(-4, 5) for b in range(-2, 3) if (a, b) != (0, 0)]
FORWARD = [(0, 0, 0), (0, 0, 1), (1, 0, -1), (1, 0, 0), (1, 0, 1)] + [
    (a, 1, c) for a in (-1, 0, 1) for c in (-1, 0, 1)
]
ALL = [(a, b, c) for b in (-1, 0, 1) for a in (-1, 0, 1) for c in (-1, 0, 1)]
BACKWARD = [o for o in ALL if o not in FORWARD]


def iota(shape, dim):
    return lax.broadcasted_iota(jnp.int32, shape, dim)


def xsh(f, by):
    if by == 0:
        return f
    return pltpu.roll(f, 7 if by == 1 else 1, f.ndim - 2)


def zsh(f, by, d):
    if by == 0:
        return f
    lane = iota(f.shape, f.ndim - 1)
    if by == 1:
        return jnp.where(lane < 128 - d, pltpu.roll(f, 128 - d, f.ndim - 1), 0.0)
    return jnp.where(lane >= d, pltpu.roll(f, d, f.ndim - 1), 0.0)


def face(a, b):
    return 1.0 + jnp.square(0.5 * (a + b))


def kernel_body(n, m, x_ref, f_ref, o_ref, s):
    gx, gy = lax.axis_index("gx"), lax.axis_index("gy")

    def device(a, b):
        return (lax.rem(gx + a + n, n), lax.rem(gy + b + m, m))

    started = []

    def send(src, dst, number, a, b):
        copy = pltpu.make_async_remote_copy(
            src_ref=src,
            dst_ref=dst,
            send_sem=s.ssem.at[number],
            recv_sem=s.rsem.at[number],
            device_id=device(a, b),
            device_id_type=MESH,
        )
        copy.start()
        started.append(copy)
        return copy

    def inside(first, shape, width):
        rows = gy * width + first + iota(shape, 0)
        return (rows >= 0) & (rows < m * width)

    barrier = pltpu.get_barrier_semaphore()
    for a, b in GREETED:
        pl.semaphore_signal(barrier, inc=1, device_id=device(a, b), device_id_type=MESH)

    lane = iota((16, 128), 1)
    low = lane < 64
    take_a = jnp.where(low, 2 * lane, 2 * lane - 127)
    take_b = jnp.where(low, 2 * lane + 1, 2 * lane - 128)
    for ref, split in ((x_ref, s.split_u), (f_ref, s.split_f)):
        for x in range(8):
            va = jnp.take_along_axis(ref[x, :, 0:128], take_a, axis=1, mode="promise_in_bounds")
            vb = jnp.take_along_axis(ref[x, :, 128:256], take_b, axis=1, mode="promise_in_bounds")
            place = ((x % 2) * 4 + x // 2) * 16
            split[0, place : place + 16, :] = jnp.where(low, va, vb)
            split[1, place : place + 16, :] = pltpu.roll(jnp.where(low, vb, va), 64, 1)
    for z in range(2):
        for y in range(16):
            u = s.split_u[z, pl.ds(y, 8, stride=16), :]
            f = s.split_f[z, pl.ds(y, 8, stride=16), :]
            s.cu[z, 4 + y] = u
            s.cf[z, 4 + y] = f
    for side, at in ((0, 2), (1, 0)):
        for z in range(2):
            s.px[side, z, :, 0:2, :] = s.cu[z, 4:20, at : at + 2, :]
            s.px[side, z, :, 2:4, :] = s.cu[z, 4:20, at + 4 : at + 6, :]
            s.px[side, z, :, 4:6, :] = s.cf[z, 4:20, at : at + 2, :]
            s.px[side, z, :, 6:8, :] = s.cf[z, 4:20, at + 4 : at + 6, :]
    pl.semaphore_wait(barrier, len(GREETED))

    source_rows = {-1: pl.ds(0, 4), 0: pl.ds(0, 16), 1: pl.ds(12, 4)}
    target_rows = {-1: pl.ds(20, 4), 0: pl.ds(4, 16), 1: pl.ds(0, 4)}
    round1 = []
    number = 0
    for a in (1, -1):
        side = 0 if a == 1 else 1
        for b in (0, 1, -1):
            round1.append(
                send(
                    s.px.at[side, :, source_rows[b]],
                    s.rx.at[side, :, target_rows[b]],
                    number,
                    a,
                    b,
                )
            )
            number += 1
    for b in (1, -1):
        here = pl.ds(16, 4) if b == 1 else pl.ds(4, 4)
        for ref in (s.cu, s.cf):
            round1.append(send(ref.at[:, here], ref.at[:, target_rows[b]], number, 0, b))
            number += 1
    for copy in round1:
        copy.wait_recv()

    def assemble(i, carry):
        at = pl.ds(4 * i, 4)
        keep = inside(4 * i - 4, (4, 8, 128), 16)
        sub = iota((4, 8, 128), 1)
        for z in range(2):
            lo, mid_u, mid_f, hi = s.rx[0, z, at], s.cu[z, at], s.cf[z, at], s.rx[1, z, at]
            for x in range(2):
                for base, mid, ref in ((0, mid_u, s.u), (4, mid_f, s.f)):
                    a = base + 2 * x
                    left = pltpu.roll(lo, (8 - a) % 8, 1) if a else lo
                    here = pltpu.roll(mid, (2 - 4 * x) % 8, 1)
                    right = pltpu.roll(hi, (6 - a) % 8, 1) if (6 - a) % 8 else hi
                    value = jnp.where(sub < 2, left, jnp.where(sub < 6, here, right))
                    ref[2 * z + x, at] = jnp.where(keep, value, 0.0)
        return carry

    lax.fori_loop(0, 6, assemble, 0)
    s.u[:, 24:26] = jnp.zeros((4, 2, 8, 128), F32)

    def faces(i, carry):
        at, above = pl.ds(2 * i, 2), pl.ds(2 * i + 1, 2)
        u = [s.u[p, at] for p in range(4)]
        un = [s.u[p, above] for p in range(4)]
        keep = inside(2 * i - 4, (2, 8, 128), 16)
        first = iota((2, 8, 128), 2) == 0
        sx, sz, szd, ky = [], [], [], []
        for z in range(2):
            ka, kb = face(u[2 * z], u[2 * z + 1]), face(u[2 * z + 1], xsh(u[2 * z], 1))
            s.kx[z, at], s.kx[2 + z, at] = ka, kb
            sx.append(0.25 * (ka + kb))
        for x in range(2):
            ka, kb = face(u[x], u[2 + x]), face(u[2 + x], zsh(u[x], 1, 1))
            s.kz[x, at], s.kz[2 + x, at] = ka, kb
            sz.append(0.25 * (ka + kb))
            szd.append(jnp.where(first, face(u[x], 0.0), zsh(sz[x], -1, 1)))
        for p in range(4):
            ky.append(face(u[p], un[p]))
            s.ky[p, at] = ky[p]

        def mx(f0, f1):
            return f0 + 0.25 * (f1 + xsh(f1, -1)), 0.25 * f1

        def mz(f0, f1):
            return f0 + 0.25 * (f1 + zsh(f1, -1, 1)), 0.25 * f1

        sx0, sxp = mz(sx[0], sx[1])
        t0, tp = mx(sz[0], sz[1])
        d0, dp = mx(szd[0], szd[1])
        for k, value in enumerate((sx0, sxp, t0, tp, t0 + d0, tp + dp)):
            s.g[k, at] = jnp.where(keep, value, 0.0)
        h0, hp = mx(ky[0], ky[1])
        j0, jp = mx(ky[2], ky[3])
        h00, h0p = mz(h0, j0)
        hp0, hpp = mz(hp, jp)
        for k, value in enumerate((h00, h0p, hp0, hpp)):
            s.h[k, at] = value
        return carry

    lax.fori_loop(0, 12, faces, 0)

    def beside(ref, row, k):
        at = pl.ds(row, k)
        v = [ref[p, at] for p in range(4)]
        out = []
        for z in range(2):
            for x in range(2):
                p = 2 * z + x
                ka, kb = s.kx[z, at], s.kx[2 + z, at]
                w = v[2 * z + 1 - x]
                if x == 0:
                    total = ka * w + xsh(kb * w, -1)
                else:
                    total = ka * w + kb * xsh(w, 1)
                ka, kb = s.kz[x, at], s.kz[2 + x, at]
                w = v[2 * (1 - z) + x]
                if z == 0:
                    total += ka * w + zsh(kb * w, -1, 1)
                else:
                    total += ka * w + kb * zsh(w, 1, 1)
                total += s.ky[p, at] * ref[p, pl.ds(row + 1, k)]
                total += s.ky[p, pl.ds(row - 1, k)] * ref[p, pl.ds(row - 1, k)]
                out.append(total)
        return v, out

    def smooth0(i, carry):
        row = 2 + 2 * i
        at = pl.ds(row, 2)
        keep = inside(row - 4, (2, 8, 128), 16)
        first = iota((2, 8, 128), 2) == 0
        v, total = beside(s.u, row, 2)
        for z in range(2):
            for x in range(2):
                p = 2 * z + x
                ka, kb = s.kx[z, at], s.kx[2 + z, at]
                diag = ka + (xsh(kb, -1) if x == 0 else kb)
                ka, kb = s.kz[x, at], s.kz[2 + x, at]
                if z == 0:
                    diag += ka + jnp.where(first, face(v[p], 0.0), zsh(kb, -1, 1))
                else:
                    diag += ka + kb
                diag += s.ky[p, at] + s.ky[p, pl.ds(row - 1, 2)]
                newton = s.f[p, at] - (diag * v[p] - total[p])
                weight = WEIGHT / diag
                s.f[p, at] = newton
                s.d0[p, at] = diag
                s.w0[p, at] = weight
                s.e0[p, at] = jnp.where(keep, weight * newton, 0.0)
        return carry

    lax.fori_loop(0, 10, smooth0, 0)

    def residual0(i, carry):
        row = 3 + 2 * i
        at = pl.ds(row, 2)
        keep = inside(row - 4, (2, 8, 128), 16)
        v, total = beside(s.e0, row, 2)
        r = [s.f[p, at] - (s.d0[p, at] * v[p] - total[p]) for p in range(4)]
        r = [r[x] + 0.5 * (r[2 + x] + zsh(r[2 + x], -1, 1)) for x in range(2)]
        s.r0[at] = jnp.where(keep, r[0] + 0.5 * (r[1] + xsh(r[1], -1)), 0.0)
        return carry

    lax.fori_loop(0, 9, residual0, 0)

    def level1(i, only_up):
        base = 2 * i
        edge = (gy == 0) & (i == 2)
        keep = inside(i - 2, (1, 8, 128), 8)[0]

        def v_of(q, row):
            return 0.25 * (s.h[q, row] + s.h[q, row + 1])

        v = [v_of(q, base) for q in range(4)]
        up = [0.25 * s.g[k, base + 1] for k in range(6)]
        sx0, sxp, t0, tp, p0, pp = up
        arrays = {
            (0, 0): sx0 + xsh(sx0, -1) + p0 - v[0],
            (0, 1): sxp + xsh(sxp, -1) - t0 - v[1],
            (1, 0): pp - sx0 - v[2],
            (1, 1): -sxp - tp - v[3],
        }
        fill(9, i, arrays, keep)
        if only_up:
            return
        vd = [jnp.where(edge, s.h[q, base - 1], v_of(q, base - 2)) for q in range(4)]
        both = [v[q] + vd[q] for q in range(4)]
        sx0, sxp, t0, tp, p0, pp = [
            s.g[k, base] + up[k] + 0.25 * s.g[k, base - 1] for k in range(6)
        ]
        arrays = {
            (0, 0): sx0 + xsh(sx0, -1) + p0 + both[0],
            (0, 1): sxp + xsh(sxp, -1) - t0 + both[1],
            (1, 0): pp - sx0 + both[2],
            (1, 1): both[3] - sxp - tp,
        }
        fill(0, i, arrays, keep)
        s.w1[i] = jnp.where(keep, WEIGHT / arrays[(0, 0)], 0.0)

    def fill(first, i, arrays, keep):
        for key in arrays:
            arrays[key] = jnp.where(keep, arrays[key], 0.0)
        for a in (-1, 0, 1):
            for c in (-1, 0, 1):
                value = zsh(arrays[(abs(a), abs(c))], min(c, 0), 1)
                s.a1[first + 3 * (a + 1) + c + 1, i] = xsh(value, min(a, 0))

    def coefficient1(o, row, k):
        a, b, c = o
        at = 3 * (a + 1) + c + 1
        if b == 0:
            return s.a1[at, pl.ds(row, k)]
        return s.a1[9 + at, pl.ds(row if b == 1 else row - 1, k)]

    level1(0, True)

    def level1_step(i, carry):
        level1(i, False)
        return carry

    lax.fori_loop(1, 11, level1_step, 0)

    sub = iota((8, 128), 0)

    def start1(y, carry):
        row = 4 + 2 * y
        b1 = s.r0[row] + 0.5 * (s.r0[row - 1] + s.r0[row + 1])
        e1 = s.w1[y + 2] * b1
        s.re1[1, y + 2] = jnp.where(sub < 4, pltpu.roll(e1, 6, 0), pltpu.roll(b1, 2, 0))
        return carry

    lax.fori_loop(0, 8, start1, 0)

    mine = {-1: pl.ds(2, 2), 0: pl.ds(2, 8), 1: pl.ds(8, 2)}
    theirs = {-1: pl.ds(10, 2), 0: pl.ds(2, 8), 1: pl.ds(0, 2)}
    round2 = []
    for a, b in AROUND:
        round2.append(send(s.re1.at[1, mine[b]], s.re1.at[1 - a, theirs[b]], number, a, b))
        number += 1

    def coarsen(coefficient, row, d, store):
        def get(o, r):
            return coefficient(o, r, 1)[0]

        y0, y1 = {}, {}
        for a in (-1, 0, 1):
            for c in (-1, 0, 1):
                zero_up = 0.25 * get((a, 0, c), row + 1)
                plus = get((a, 1, c), row)
                y0[a, c] = (
                    get((a, 0, c), row)
                    + zero_up
                    + 0.25 * get((a, 0, c), row - 1)
                    + 0.5
                    * (
                        get((a, -1, c), row)
                        + get((a, -1, c), row + 1)
                        + plus
                        + get((a, 1, c), row - 1)
                    )
                )
                y1[a, c] = 0.5 * (plus + get((a, 1, c), row + 1)) + zero_up

        def three(lo, mid, hi, shift, want):
            out = {}
            q = 0.25 * mid
            lo, hi = 0.5 * lo, 0.5 * hi
            if 0 in want:
                out[0] = mid + lo + hi + shift(q + lo, 1) + shift(q + hi, -1)
            if 1 in want:
                out[1] = hi + shift(q + hi, 1)
            if -1 in want:
                out[-1] = lo + shift(q + lo, -1)
            return out

        def by_z(f, by):
            return zsh(f, by, d)

        for b, table in ((0, y0), (1, y1)):
            xs = {}
            for c in (-1, 0, 1):
                want = (0, 1) if b == 0 else (-1, 0, 1)
                got = three(table[-1, c], table[0, c], table[1, c], xsh, want)
                for a in got:
                    xs[a, c] = got[a]
            for a in (0, 1) if b == 0 else (-1, 0, 1):
                want = (0, 1) if (a, b) == (0, 0) else (-1, 0, 1)
                got = three(xs[a, -1], xs[a, 0], xs[a, 1], by_z, want)
                for c in got:
                    store(FORWARD.index((a, b, c)), got[c])

    def coarsen1(y, carry):
        def store(k, value):
            s.ra2[1, y + 2, k // 4, 2 * (k % 4) : 2 * (k % 4) + 1, :] = value[2:3]
            s.ra2[1, y + 2, k // 4, 2 * (k % 4) + 1 : 2 * (k % 4) + 2, :] = value[4:5]
            if k == 0:
                s.w2own[y] = WEIGHT / value

        coarsen(coefficient1, 2 * y + 2, 1, store)
        return carry

    lax.fori_loop(0, 4, coarsen1, 0)
    mine = {-1: pl.ds(2, 2), 0: pl.ds(2, 4), 1: pl.ds(4, 2)}
    theirs = {-1: pl.ds(6, 2), 0: pl.ds(2, 4), 1: pl.ds(0, 2)}
    round2a = []
    for a, b in AROUND:
        round2a.append(send(s.ra2.at[1, mine[b]], s.ra2.at[1 - a, theirs[b]], number, a, b))
        number += 1
    for b in (-1, 0, 1):
        round2a.append(send(s.ra2.at[1, mine[b], 1], s.ra2.at[3, theirs[b], 1], number, -2, b))
        number += 1

    for copy in round2:
        copy.wait_recv()

    def unpack1(i, carry):
        at = pl.ds(2 * i, 2)
        keep = inside(2 * i - 2, (2, 8, 128), 8)
        sub = iota((2, 8, 128), 1)
        lo, mid, hi = s.re1[0, at], s.re1[1, at], s.re1[2, at]
        e = jnp.where(
            sub < 2,
            pltpu.roll(lo, 6, 1),
            jnp.where(sub < 6, pltpu.roll(mid, 2, 1), pltpu.roll(hi, 6, 1)),
        )
        b = jnp.where(
            sub < 2,
            pltpu.roll(lo, 2, 1),
            jnp.where(sub < 6, pltpu.roll(mid, 6, 1), pltpu.roll(hi, 2, 1)),
        )
        s.e1[at] = jnp.where(keep, e, 0.0)
        s.b1[at] = jnp.where(keep, b, 0.0)
        return carry

    lax.fori_loop(0, 6, unpack1, 0)

    def apply(coefficient, ref, row, k, d):
        total = None
        for b in (-1, 0, 1):
            e = ref[pl.ds(row + b, k)]
            for c in (-1, 0, 1):
                ez = zsh(e, c, d)
                for a in (-1, 0, 1):
                    term = coefficient((a, b, c), row, k) * xsh(ez, a)
                    total = term if total is None else total + term
        return total

    def gather_zx(r, d):
        r = r + 0.5 * (zsh(r, -1, d) + zsh(r, 1, d))
        return r + 0.5 * (xsh(r, -1) + xsh(r, 1))

    def residual1(i, carry):
        row = 1 + i
        keep = inside(row - 2, (1, 8, 128), 8)
        r = s.b1[pl.ds(row, 1)] - apply(coefficient1, s.e1, row, 1, 1)
        s.r1[pl.ds(row, 1)] = jnp.where(keep, gather_zx(r, 1), 0.0)
        return carry

    lax.fori_loop(0, 9, residual1, 0)

    def start2(y, carry):
        row = 2 * y + 2
        b2 = s.r1[row] + 0.5 * (s.r1[row - 1] + s.r1[row + 1])
        e2 = s.w2own[y] * b2
        s.re2[1, y + 2, 0:1, :] = e2[2:3]
        s.re2[1, y + 2, 1:2, :] = e2[4:5]
        s.re2[1, y + 2, 2:3, :] = b2[2:3]
        s.re2[1, y + 2, 3:4, :] = b2[4:5]
        return carry

    lax.fori_loop(0, 4, start2, 0)

    mine = {-1: pl.ds(2, 3), 0: pl.ds(2, 4), 1: pl.ds(4, 2)}
    theirs = {-1: pl.ds(6, 3), 0: pl.ds(2, 4), 1: pl.ds(0, 2)}
    round3 = []
    for a, b in AROUND + [(-2, -1), (-2, 0), (-2, 1)]:
        round3.append(send(s.re2.at[1, mine[b]], s.re2.at[1 - a, theirs[b]], number, a, b))
        number += 1

    for copy in round2a:
        copy.wait_recv()

    def unpack_a2(i, carry):
        at = pl.ds(2 * i, 2)
        keep = inside(2 * i - 2, (2, 8, 128), 4)
        sub = iota((2, 8, 128), 1)
        for t in range(4):
            lo, mid, hi = s.ra2[0, at, t], s.ra2[1, at, t], s.ra2[2, at, t]
            for j in range(4):
                k = 4 * t + j
                if k >= 14:
                    continue

                def rolled(v, to):
                    by = (to - 2 * j) % 8
                    return pltpu.roll(v, by, 1) if by else v

                value = jnp.where(sub < 4, rolled(mid, 2), rolled(hi, 4))
                if t == 1:
                    value = jnp.where(sub < 6, value, rolled(s.ra2[3, at, 1], 6))
                value = jnp.where(sub < 2, rolled(lo, 0), value)
                value = jnp.where(keep, value, 0.0)
                s.a2[k, at] = value
                if k == 0:
                    s.w2[at] = jnp.where(keep, WEIGHT / value, 0.0)
        return carry

    lax.fori_loop(0, 4, unpack_a2, 0)

    def expand(ref, back, row, d):
        for k, (a, b, c) in enumerate(BACKWARD):
            value = ref[FORWARD.index((-a, -b, -c)), pl.ds(row + b, 1)]
            back[k, pl.ds(row, 1)] = xsh(zsh(value, c, d), a)

    def reader(ref, back):
        def coefficient(o, row, k):
            if o in FORWARD:
                return ref[FORWARD.index(o), pl.ds(row, k)]
            return back[BACKWARD.index(o), pl.ds(row, k)]

        return coefficient

    def expand2(i, carry):
        expand(s.a2, s.a2b, i, 2)
        return carry

    lax.fori_loop(1, 8, expand2, 0)
    coefficient2 = reader(s.a2, s.a2b)

    def coarsen2(y, carry):
        def store(k, value):
            s.a3own[k, y] = value

        coarsen(coefficient2, 2 * y + 2, 2, store)
        return carry

    lax.fori_loop(0, 2, coarsen2, 0)
    lane = iota((8, 128), 1)
    own = pl.ds(24, 8)
    for y in range(2):
        for q in range(4):
            value = s.a3own[4 * q, y]
            for j in range(1, 4):
                if 4 * q + j < 14:
                    other = pltpu.roll(s.a3own[4 * q + j, y], j, 1)
                    value = jnp.where(lane % 4 == j, other, value)
            s.ra3[2, 24 + 4 * y + q : 25 + 4 * y + q, :] = value[2:3]

    def send_wide(ref, number):
        copies = []
        for a, b in WIDE:
            copies.append(send(ref.at[2, own], ref.at[2 + b, pl.ds(8 * (a + 3), 8)], number, -a, -b))
            number += 1
        return copies, number

    round3a, number = send_wide(s.ra3, number)

    for copy in round3:
        copy.wait_recv()
    for k in range(4):
        at = slice(2 * k, 2 * k + 2)
        keep = inside(-2, (9, 2, 128), 4)
        s.e2[0:9, at, :] = jnp.where(keep, s.re2[k, 0:9, 0:2, :], 0.0)
        s.b2[0:9, at, :] = jnp.where(keep, s.re2[k, 0:9, 2:4, :], 0.0)

    def residual2(i, carry):
        row = 1 + i
        keep = inside(row - 2, (1, 8, 128), 4)
        r = s.b2[pl.ds(row, 1)] - apply(coefficient2, s.e2, row, 1, 2)
        s.r2[pl.ds(row, 1)] = jnp.where(keep, gather_zx(r, 2), 0.0)
        return carry

    lax.fori_loop(0, 5, residual2, 0)
    for y in range(2):
        row = 2 * y + 2
        b3 = s.r2[row] + 0.5 * (s.r2[row - 1] + s.r2[row + 1])
        e3 = WEIGHT * b3 / s.a3own[0, y]
        s.rb3[2, 24 + y : 25 + y, :] = b3[2:3]
        s.rb3[2, 26 + y : 27 + y, :] = e3[2:3]

    round4, number = send_wide(s.rb3, number)
    for copy in round3a:
        copy.wait_recv()

    for dy in range(5):
        for y in range(2):
            row = 2 * dy + y
            keep = inside(row - 4, (1, 8, 128), 2)[0]
            for q in range(4):
                value = jnp.where(keep, s.ra3[dy, pl.ds(4 * y + q, 8, stride=8), :], 0.0)
                for j in range(4):
                    if 4 * q + j < 14:
                        s.a3[4 * q + j, row] = pltpu.roll(value, 128 - j, 1) if j else value
            s.w3[row] = jnp.where(keep, WEIGHT / s.a3[0, row], 0.0)

    def expand3(i, carry):
        expand(s.a3, s.a3b, i, 4)
        return carry

    lax.fori_loop(2, 9, expand3, 0)
    coefficient3 = reader(s.a3, s.a3b)

    for copy in round4:
        copy.wait_recv()
    for dy in range(5):
        for y in range(2):
            row = 2 * dy + y
            keep = inside(row - 4, (1, 8, 128), 2)[0]
            b3 = s.rb3[dy, pl.ds(y, 8, stride=8), :]
            e3 = s.rb3[dy, pl.ds(2 + y, 8, stride=8), :]
            s.b3[row] = jnp.where(keep, b3, 0.0)
            s.e3[0, row] = jnp.where(keep, e3, 0.0)

    def sweep(source, target, low, high):
        def step(row, carry):
            at = pl.ds(row, 1)
            old, new = s.e3.at[source], s.e3.at[target]
            r = s.b3[at] - apply(coefficient3, old, row, 1, 4)
            new[at] = old[at] + s.w3[at] * r
            return carry

        lax.fori_loop(low + 4, high + 5, step, 0)

    sweep(0, 1, -2, 3)
    sweep(1, 0, -1, 2)
    sweep(0, 1, 0, 1)
    for y in range(2):
        s.re3[2, 24 + y : 25 + y, :] = s.e3[1, 4 + y, 3:4, :]

    round5, number = send_wide(s.re3, number)
    for copy in round5:
        copy.wait_recv()
    for dy in range(5):
        for y in range(2):
            row = 2 * dy + y
            keep = inside(row - 4, (1, 8, 128), 2)[0]
            e3 = s.re3[dy, pl.ds(y, 8, stride=8), :]
            s.e3[0, row] = jnp.where(keep, e3, 0.0)
    sweep(0, 1, -2, 4)
    sweep(1, 0, -1, 3)

    def spread(c, first, d, place):
        rows = c.shape[0]
        half = 0.5 * (c + xsh(c, 1))
        for k in range(4):
            place[0:rows, 2 * k : 2 * k + 1, :] = c[:, first + k : first + k + 1]
            place[0:rows, 2 * k + 1 : 2 * k + 2, :] = half[:, first + k : first + k + 1]
        value = place[0:rows]
        coarse = iota(value.shape, 2) % (2 * d) == 0
        place[0:rows] = jnp.where(coarse, value, 0.5 * (zsh(value, -1, d) + zsh(value, 1, d)))

    def add_rows(place, rows, target, width):
        for i in range(rows):
            value = place[i // 2]
            if i % 2:
                value = 0.5 * (value + place[i // 2 + 1])
            keep = inside(i - 2, (1, 8, 128), width)[0]
            target[i] = target[i] + jnp.where(keep, value, 0.0)

    spread(s.e3[0, 3:8], 2, 2, s.place)
    add_rows(s.place, 9, s.e2, 4)

    def post2(row, carry):
        at = pl.ds(row, 1)
        r = s.b2[at] - apply(coefficient2, s.e2, row, 1, 2)
        s.x2[at] = s.e2[at] + s.w2[at] * r
        return carry

    lax.fori_loop(1, 8, post2, 0)
    spread(s.x2[1:8], 1, 1, s.place)
    add_rows(s.place, 12, s.e1, 8)

    def post1(i, carry):
        row = 1 + i
        at = pl.ds(row, 1)
        r = s.b1[at] - apply(coefficient1, s.e1, row, 1, 1)
        s.x1[at] = s.e1[at] + s.w1[at] * r
        return carry

    lax.fori_loop(0, 10, post1, 0)
    s.x1[11] = jnp.zeros((8, 128), F32)

    def prolong0(i, carry):
        c = s.x1[i]
        for step in range(2):
            row = 2 * i + step
            keep = inside(row - 4, (1, 8, 128), 16)[0]
            if step:
                c = 0.5 * (c + s.x1[i + 1])
            cz = 0.5 * (c + zsh(c, 1, 1))
            values = (c, 0.5 * (c + xsh(c, 1)), cz, 0.5 * (cz + xsh(cz, 1)))
            for p in range(4):
                s.e0[p, row] = s.e0[p, row] + jnp.where(keep, values[p], 0.0)
        return carry

    lax.fori_loop(1, 11, prolong0, 0)

    def finish(i, carry):
        row = 4 + 2 * i
        at = pl.ds(row, 2)
        v, total = beside(s.e0, row, 2)
        sub = iota((2, 8, 128), 1)
        for z in range(2):
            done = []
            for x in range(2):
                p = 2 * z + x
                r = s.f[p, at] - (s.d0[p, at] * v[p] - total[p])
                value = s.u[p, at] + (v[p] + s.w0[p, at] * r)
                done.append(pltpu.roll(value, 6 if x == 0 else 2, 1))
            both = jnp.where(sub < 4, done[0], done[1])
            for k in range(2):
                s.co[z, pl.ds(pl.multiple_of(16 * i + 8 * k, 8), 8), :] = both[k]
        return carry

    lax.fori_loop(0, 8, finish, 0)

    lane = iota((16, 128), 1)
    low = lane < 64
    take = jnp.where(lane % 2 == 0, lane // 2, 64 + lane // 2)
    for x in range(8):
        place = (x % 2) * 4 + x // 2
        even = s.co[0, pl.ds(place, 16, stride=8), :]
        odd = pltpu.roll(s.co[1, pl.ds(place, 16, stride=8), :], 64, 1)
        va, vb = jnp.where(low, even, odd), pltpu.roll(jnp.where(low, odd, even), 64, 1)
        o_ref[x, :, 0:128] = jnp.take_along_axis(va, take, axis=1, mode="promise_in_bounds")
        o_ref[x, :, 128:256] = jnp.take_along_axis(vb, take, axis=1, mode="promise_in_bounds")
    for copy in started:
        copy.wait_send()


COPIES = 10 + 8 + 11 + 11 + 3 * len(WIDE)
TILE = (8, 128)
SHAPES = {
    "split_u": (2, 128, 128),
    "split_f": (2, 128, 128),
    "co": (2, 128, 128),
    "cu": (2, 24) + TILE,
    "cf": (2, 24) + TILE,
    "px": (2, 2, 16) + TILE,
    "rx": (2, 2, 24) + TILE,
    "u": (4, 26) + TILE,
    "f": (4, 26) + TILE,
    "kx": (4, 24) + TILE,
    "kz": (4, 24) + TILE,
    "ky": (4, 24) + TILE,
    "g": (6, 24) + TILE,
    "h": (4, 24) + TILE,
    "d0": (4, 24) + TILE,
    "w0": (4, 24) + TILE,
    "e0": (4, 26) + TILE,
    "r0": (24,) + TILE,
    "a1": (18, 12) + TILE,
    "w1": (12,) + TILE,
    "re1": (3, 12) + TILE,
    "e1": (12,) + TILE,
    "b1": (12,) + TILE,
    "x1": (12,) + TILE,
    "r1": (12,) + TILE,
    "ra2": (4, 8, 4) + TILE,
    "w2own": (4,) + TILE,
    "a2": (14, 8) + TILE,
    "a2b": (13, 8) + TILE,
    "w2": (8,) + TILE,
    "re2": (4, 9) + TILE,
    "e2": (9,) + TILE,
    "b2": (9,) + TILE,
    "x2": (9,) + TILE,
    "r2": (9,) + TILE,
    "a3own": (14, 2) + TILE,
    "ra3": (5, 64, 128),
    "rb3": (5, 64, 128),
    "re3": (5, 64, 128),
    "a3": (14, 10) + TILE,
    "a3b": (13, 10) + TILE,
    "w3": (10,) + TILE,
    "b3": (10,) + TILE,
    "e3": (2, 10) + TILE,
    "place": (8,) + TILE,
}


class Scratch:
    pass


def on_device(n, m, state, forcing):
    names = list(SHAPES)

    def body(x_ref, f_ref, o_ref, *scratch):
        s = Scratch()
        for name, ref in zip(names, scratch):
            setattr(s, name, ref)
        s.ssem, s.rsem = scratch[len(names) :]
        kernel_body(n, m, x_ref, f_ref, o_ref, s)

    return pl.pallas_call(
        body,
        out_shape=jax.ShapeDtypeStruct(state.shape, F32),
        in_specs=[pl.BlockSpec(memory_space=pltpu.VMEM)] * 2,
        out_specs=pl.BlockSpec(memory_space=pltpu.VMEM),
        scratch_shapes=[pltpu.VMEM(shape, F32) for shape in SHAPES.values()]
        + [pltpu.SemaphoreType.DMA((COPIES,))] * 2,
        compiler_params=pltpu.CompilerParams(
            collective_id=0, has_side_effects=True, vmem_limit_bytes=48 << 20
        ),
    )(state, forcing)


def solution(mesh):
    n, m = mesh.shape["gx"], mesh.shape["gy"]
    return jax.shard_map(
        lambda state, forcing: on_device(n, m, state, forcing),
        mesh=mesh,
        in_specs=(P("gx", "gy", None), P("gx", "gy", None)),
        out_specs=P("gx", "gy", None),
        check_vma=False,
    )
```

time: 403 us -> 65.3 us (0.16)
  the two profiles are of different devices: /device:TPU:6 before, /device:TPU:1 now
where the time goes in v1:
time: 65.3 us; the launch traced here: 65.2 us
  Pallas kernels  62.7 us (96%)
  local copies, waits for them, and re-layouts  2.47 us (4%)
    pallas_call x1, Pallas kernels, on_device(): pl.pallas_call(body, out_shape=jax.ShapeDtypeStruct(state.shape, F32), in...  62.7 us
    unnamed x5, local copies, waits for them, and re-layouts  2.47 us

profile of v1, /device:TPU:1, one launch (start us, length us, event | category | flops | bytes accessed | tf_op | source)
XLA Modules:
  0.0 65.2 jit_solution(16791716387256029137)
XLA Ops:
  0.0 0.0 copy-start
  0.0 0.9 %copy-done = f32[8,16,256]{2,1,0:T(8,128)S(1)} copy-done((f32[8,16,256]{2,1,0:T(8,128)S(1)}, f32[8,16,256]{2,1,0:T(8,128)}, u32[]{:S(2)}) %copy-start) | copy-done | bytes 131096
  0.9 0.0 copy-start.1
  0.9 0.9 %copy-done.1 = f32[8,16,256]{2,1,0:T(8,128)S(1)} copy-done((f32[8,16,256]{2,1,0:T(8,128)S(1)}, f32[8,16,256]{2,1,0:T(8,128)}, u32[]{:S(2)}) %copy-start.1) | copy-done | bytes 131096
  1.8 62.7 %shard_map.28 = f32[8,16,256]{2,1,0:T(8,128)S(1)} custom-call(f32[8,16,256]{2,1,0:T(8,128)S(1)} %copy-done, f32[8,16,256]{2,1,0:T(8,128)S(1)} %copy-done.1), custom_call_target="tpu_custom_call" | custom-call | tf_op jit(solution)/shard_map/pallas_call | solution.py:777
  64.5 0.7 %copy.4 = f32[8,16,256]{2,1,0:T(8,128)} copy(f32[8,16,256]{2,1,0:T(8,128)S(1)} %shard_map.28) | data formatting | bytes 262144
Async XLA Ops:
  0.0 0.9 %copy-start = (f32[8,16,256]{2,1,0:T(8,128)S(1)}, f32[8,16,256]{2,1,0:T(8,128)}, u32[]{:S(2)}) copy-start(f32[8,16,256]{2,1,0:T(8,128)} %x_ref.1) | copy-start | bytes 393220
  0.9 0.9 %copy-start.1 = (f32[8,16,256]{2,1,0:T(8,128)S(1)}, f32[8,16,256]{2,1,0:T(8,128)}, u32[]{:S(2)}) copy-start(f32[8,16,256]{2,1,0:T(8,128)} %f_ref.1) | copy-start | bytes 393220

commit v2 on v1

--- a/solution.py
+++ b/solution.py
@@ -10,8 +10,9 @@
 F32 = jnp.float32
 
 AROUND = [(a, b) for a in (-1, 0, 1) for b in (-1, 0, 1) if (a, b) != (0, 0)]
+GREETED = AROUND + [(2, 0)]
 WIDE = [(a, b) for a in range(-3, 5) for b in range(-2, 3) if (a, b) != (0, 0)]
-GREETED = [(a, b) for a in range(-4, 5) for b in range(-2, 3) if (a, b) != (0, 0)]
+ROUND1 = [(1, 1), (1, -1), (-1, 1), (-1, -1), (0, 1), (0, -1), (1, 0), (-1, 0)]
 FORWARD = [(0, 0, 0), (0, 0, 1), (1, 0, -1), (1, 0, 0), (1, 0, 1)] + [
     (a, 1, c) for a in (-1, 0, 1) for c in (-1, 0, 1)
 ]
@@ -71,73 +72,64 @@
     for a, b in GREETED:
         pl.semaphore_signal(barrier, inc=1, device_id=device(a, b), device_id_type=MESH)
 
-    lane = iota((16, 128), 1)
-    low = lane < 64
-    take_a = jnp.where(low, 2 * lane, 2 * lane - 127)
-    take_b = jnp.where(low, 2 * lane + 1, 2 * lane - 128)
-    for ref, split in ((x_ref, s.split_u), (f_ref, s.split_f)):
-        for x in range(8):
-            va = jnp.take_along_axis(ref[x, :, 0:128], take_a, axis=1, mode="promise_in_bounds")
-            vb = jnp.take_along_axis(ref[x, :, 128:256], take_b, axis=1, mode="promise_in_bounds")
-            place = ((x % 2) * 4 + x // 2) * 16
-            split[0, place : place + 16, :] = jnp.where(low, va, vb)
-            split[1, place : place + 16, :] = pltpu.roll(jnp.where(low, vb, va), 64, 1)
-    for z in range(2):
-        for y in range(16):
-            u = s.split_u[z, pl.ds(y, 8, stride=16), :]
-            f = s.split_f[z, pl.ds(y, 8, stride=16), :]
-            s.cu[z, 4 + y] = u
-            s.cf[z, 4 + y] = f
-    for side, at in ((0, 2), (1, 0)):
-        for z in range(2):
-            s.px[side, z, :, 0:2, :] = s.cu[z, 4:20, at : at + 2, :]
-            s.px[side, z, :, 2:4, :] = s.cu[z, 4:20, at + 4 : at + 6, :]
-            s.px[side, z, :, 4:6, :] = s.cf[z, 4:20, at : at + 2, :]
-            s.px[side, z, :, 6:8, :] = s.cf[z, 4:20, at + 4 : at + 6, :]
+    here_x = {-1: pl.ds(0, 4), 0: pl.ds(0, 8), 1: pl.ds(4, 4)}
+    there_x = {-1: pl.ds(12, 4), 0: pl.ds(4, 8), 1: pl.ds(0, 4)}
+    here_y = {-1: pl.ds(0, 4), 0: pl.ds(0, 16), 1: pl.ds(12, 4)}
+    there_y = {-1: pl.ds(24, 4), 0: pl.ds(8, 16), 1: pl.ds(4, 4)}
+    here_fx = {-1: pl.ds(0, 1), 0: pl.ds(0, 8), 1: pl.ds(6, 2)}
+    there_fx = {-1: pl.ds(12, 1), 0: pl.ds(4, 8), 1: pl.ds(2, 2)}
+    own = [
+        pltpu.make_async_copy(ref, raw.at[4:12, 8:24], s.lsem.at[k])
+        for k, (ref, raw) in enumerate(((x_ref, s.raw_u), (f_ref, s.raw_f)))
+    ]
+    for copy in own:
+        copy.start()
     pl.semaphore_wait(barrier, len(GREETED))
-
-    source_rows = {-1: pl.ds(0, 4), 0: pl.ds(0, 16), 1: pl.ds(12, 4)}
-    target_rows = {-1: pl.ds(20, 4), 0: pl.ds(4, 16), 1: pl.ds(0, 4)}
     round1 = []
     number = 0
-    for a in (1, -1):
-        side = 0 if a == 1 else 1
-        for b in (0, 1, -1):
+    for a, b in ROUND1:
+        for ref, raw, hx, tx in (
+            (x_ref, s.raw_u, here_x, there_x),
+            (f_ref, s.raw_f, here_fx, there_fx),
+        ):
             round1.append(
-                send(
-                    s.px.at[side, :, source_rows[b]],
-                    s.rx.at[side, :, target_rows[b]],
-                    number,
-                    a,
-                    b,
-                )
+                send(ref.at[hx[a], here_y[b]], raw.at[tx[a], there_y[b]], number, a, b)
             )
             number += 1
-    for b in (1, -1):
-        here = pl.ds(16, 4) if b == 1 else pl.ds(4, 4)
-        for ref in (s.cu, s.cf):
-            round1.append(send(ref.at[:, here], ref.at[:, target_rows[b]], number, 0, b))
-            number += 1
+
+    def split(raw, out, plane, tiles):
+        for first, rows in tiles:
+            lane = iota((rows, 128), 1)
+            low = lane < 64
+            take_a = jnp.where(low, 2 * lane, 2 * lane - 127)
+            take_b = jnp.where(low, 2 * lane + 1, 2 * lane - 128)
+            va = raw[plane, first : first + rows, 0:128]
+            vb = raw[plane, first : first + rows, 128:256]
+            va = jnp.take_along_axis(va, take_a, axis=1, mode="promise_in_bounds")
+            vb = jnp.take_along_axis(vb, take_b, axis=1, mode="promise_in_bounds")
+            place = ((plane % 2) * 8 + plane // 2) * 32 + first
+            out[0, place : place + rows, :] = jnp.where(low, va, vb)
+            out[1, place : place + rows, :] = pltpu.roll(jnp.where(low, vb, va), 64, 1)
+
+    for copy in own:
+        copy.wait()
+    for x in range(4, 12):
+        split(s.raw_u, s.split_u, x, ((8, 16),))
+        split(s.raw_f, s.split_f, x, ((8, 16),))
     for copy in round1:
         copy.wait_recv()
-
-    def assemble(i, carry):
-        at = pl.ds(4 * i, 4)
-        keep = inside(4 * i - 4, (4, 8, 128), 16)
-        sub = iota((4, 8, 128), 1)
-        for z in range(2):
-            lo, mid_u, mid_f, hi = s.rx[0, z, at], s.cu[z, at], s.cf[z, at], s.rx[1, z, at]
-            for x in range(2):
-                for base, mid, ref in ((0, mid_u, s.u), (4, mid_f, s.f)):
-                    a = base + 2 * x
-                    left = pltpu.roll(lo, (8 - a) % 8, 1) if a else lo
-                    here = pltpu.roll(mid, (2 - 4 * x) % 8, 1)
-                    right = pltpu.roll(hi, (6 - a) % 8, 1) if (6 - a) % 8 else hi
-                    value = jnp.where(sub < 2, left, jnp.where(sub < 6, here, right))
-                    ref[2 * z + x, at] = jnp.where(keep, value, 0.0)
-        return carry
-
-    lax.fori_loop(0, 6, assemble, 0)
+    for x in range(16):
+        tiles = ((0, 8), (24, 8)) if 4 <= x < 12 else ((0, 32),)
+        split(s.raw_u, s.split_u, x, tiles)
+        if 2 <= x < 13:
+            split(s.raw_f, s.split_f, x, tiles)
+    for i in range(24):
+        keep = inside(i - 4, (1, 8, 128), 16)[0]
+        for p in range(4):
+            at = pl.ds((p % 2) * 256 + i + 4, 8, stride=32)
+            u = s.split_u[p // 2, at, :]
+            s.u[p, i] = u if 4 <= i < 20 else jnp.where(keep, u, 0.0)
+            s.f[p, i] = s.split_f[p // 2, at, :]
     s.u[:, 24:26] = jnp.zeros((4, 2, 8, 128), F32)
 
     def faces(i, carry):
@@ -179,7 +171,7 @@
             s.h[k, at] = value
         return carry
 
-    lax.fori_loop(0, 12, faces, 0)
+    lax.fori_loop(0, 12, faces, 0, unroll=True)
 
     def beside(ref, row, k):
         at = pl.ds(row, k)
@@ -230,7 +222,7 @@
                 s.e0[p, at] = jnp.where(keep, weight * newton, 0.0)
         return carry
 
-    lax.fori_loop(0, 10, smooth0, 0)
+    lax.fori_loop(0, 10, smooth0, 0, unroll=True)
 
     def residual0(i, carry):
         row = 3 + 2 * i
@@ -242,7 +234,7 @@
         s.r0[at] = jnp.where(keep, r[0] + 0.5 * (r[1] + xsh(r[1], -1)), 0.0)
         return carry
 
-    lax.fori_loop(0, 9, residual0, 0)
+    lax.fori_loop(0, 9, residual0, 0, unroll=True)
 
     def level1(i, only_up):
         base = 2 * i
@@ -299,7 +291,7 @@
         level1(i, False)
         return carry
 
-    lax.fori_loop(1, 11, level1_step, 0)
+    lax.fori_loop(1, 11, level1_step, 0, unroll=True)
 
     sub = iota((8, 128), 0)
 
@@ -310,7 +302,7 @@
         s.re1[1, y + 2] = jnp.where(sub < 4, pltpu.roll(e1, 6, 0), pltpu.roll(b1, 2, 0))
         return carry
 
-    lax.fori_loop(0, 8, start1, 0)
+    lax.fori_loop(0, 8, start1, 0, unroll=True)
 
     mine = {-1: pl.ds(2, 2), 0: pl.ds(2, 8), 1: pl.ds(8, 2)}
     theirs = {-1: pl.ds(10, 2), 0: pl.ds(2, 8), 1: pl.ds(0, 2)}
@@ -380,7 +372,7 @@
         coarsen(coefficient1, 2 * y + 2, 1, store)
         return carry
 
-    lax.fori_loop(0, 4, coarsen1, 0)
+    lax.fori_loop(0, 4, coarsen1, 0, unroll=True)
     mine = {-1: pl.ds(2, 2), 0: pl.ds(2, 4), 1: pl.ds(4, 2)}
     theirs = {-1: pl.ds(6, 2), 0: pl.ds(2, 4), 1: pl.ds(0, 2)}
     round2a = []
@@ -413,7 +405,7 @@
         s.b1[at] = jnp.where(keep, b, 0.0)
         return carry
 
-    lax.fori_loop(0, 6, unpack1, 0)
+    lax.fori_loop(0, 6, unpack1, 0, unroll=True)
 
     def apply(coefficient, ref, row, k, d):
         total = None
@@ -437,7 +429,7 @@
         s.r1[pl.ds(row, 1)] = jnp.where(keep, gather_zx(r, 1), 0.0)
         return carry
 
-    lax.fori_loop(0, 9, residual1, 0)
+    lax.fori_loop(0, 9, residual1, 0, unroll=True)
 
     def start2(y, carry):
         row = 2 * y + 2
@@ -449,7 +441,7 @@
         s.re2[1, y + 2, 3:4, :] = b2[4:5]
         return carry
 
-    lax.fori_loop(0, 4, start2, 0)
+    lax.fori_loop(0, 4, start2, 0, unroll=True)
 
     mine = {-1: pl.ds(2, 3), 0: pl.ds(2, 4), 1: pl.ds(4, 2)}
     theirs = {-1: pl.ds(6, 3), 0: pl.ds(2, 4), 1: pl.ds(0, 2)}
@@ -486,7 +478,7 @@
                     s.w2[at] = jnp.where(keep, WEIGHT / value, 0.0)
         return carry
 
-    lax.fori_loop(0, 4, unpack_a2, 0)
+    lax.fori_loop(0, 4, unpack_a2, 0, unroll=True)
 
     def expand(ref, back, row, d):
         for k, (a, b, c) in enumerate(BACKWARD):
@@ -505,7 +497,7 @@
         expand(s.a2, s.a2b, i, 2)
         return carry
 
-    lax.fori_loop(1, 8, expand2, 0)
+    lax.fori_loop(1, 8, expand2, 0, unroll=True)
     coefficient2 = reader(s.a2, s.a2b)
 
     def coarsen2(y, carry):
@@ -515,9 +507,9 @@
         coarsen(coefficient2, 2 * y + 2, 2, store)
         return carry
 
-    lax.fori_loop(0, 2, coarsen2, 0)
+    lax.fori_loop(0, 2, coarsen2, 0, unroll=True)
     lane = iota((8, 128), 1)
-    own = pl.ds(24, 8)
+    middle = pl.ds(24, 8)
     for y in range(2):
         for q in range(4):
             value = s.a3own[4 * q, y]
@@ -530,7 +522,7 @@
     def send_wide(ref, number):
         copies = []
         for a, b in WIDE:
-            copies.append(send(ref.at[2, own], ref.at[2 + b, pl.ds(8 * (a + 3), 8)], number, -a, -b))
+            copies.append(send(ref.at[2, middle], ref.at[2 + b, pl.ds(8 * (a + 3), 8)], number, -a, -b))
             number += 1
         return copies, number
 
@@ -551,7 +543,7 @@
         s.r2[pl.ds(row, 1)] = jnp.where(keep, gather_zx(r, 2), 0.0)
         return carry
 
-    lax.fori_loop(0, 5, residual2, 0)
+    lax.fori_loop(0, 5, residual2, 0, unroll=True)
     for y in range(2):
         row = 2 * y + 2
         b3 = s.r2[row] + 0.5 * (s.r2[row - 1] + s.r2[row + 1])
@@ -578,7 +570,7 @@
         expand(s.a3, s.a3b, i, 4)
         return carry
 
-    lax.fori_loop(2, 9, expand3, 0)
+    lax.fori_loop(2, 9, expand3, 0, unroll=True)
     coefficient3 = reader(s.a3, s.a3b)
 
     for copy in round4:
@@ -600,7 +592,7 @@
             new[at] = old[at] + s.w3[at] * r
             return carry
 
-        lax.fori_loop(low + 4, high + 5, step, 0)
+        lax.fori_loop(low + 4, high + 5, step, 0, unroll=True)
 
     sweep(0, 1, -2, 3)
     sweep(1, 0, -1, 2)
@@ -647,7 +639,7 @@
         s.x2[at] = s.e2[at] + s.w2[at] * r
         return carry
 
-    lax.fori_loop(1, 8, post2, 0)
+    lax.fori_loop(1, 8, post2, 0, unroll=True)
     spread(s.x2[1:8], 1, 1, s.place)
     add_rows(s.place, 12, s.e1, 8)
 
@@ -658,7 +650,7 @@
         s.x1[at] = s.e1[at] + s.w1[at] * r
         return carry
 
-    lax.fori_loop(0, 10, post1, 0)
+    lax.fori_loop(0, 10, post1, 0, unroll=True)
     s.x1[11] = jnp.zeros((8, 128), F32)
 
     def prolong0(i, carry):
@@ -674,7 +666,7 @@
                 s.e0[p, row] = s.e0[p, row] + jnp.where(keep, values[p], 0.0)
         return carry
 
-    lax.fori_loop(1, 11, prolong0, 0)
+    lax.fori_loop(1, 11, prolong0, 0, unroll=True)
 
     def finish(i, carry):
         row = 4 + 2 * i
@@ -693,7 +685,7 @@
                 s.co[z, pl.ds(pl.multiple_of(16 * i + 8 * k, 8), 8), :] = both[k]
         return carry
 
-    lax.fori_loop(0, 8, finish, 0)
+    lax.fori_loop(0, 8, finish, 0, unroll=True)
 
     lane = iota((16, 128), 1)
     low = lane < 64
@@ -709,16 +701,14 @@
         copy.wait_send()
 
 
-COPIES = 10 + 8 + 11 + 11 + 3 * len(WIDE)
+COPIES = 16 + 8 + 11 + 11 + 3 * len(WIDE)
 TILE = (8, 128)
 SHAPES = {
-    "split_u": (2, 128, 128),
-    "split_f": (2, 128, 128),
+    "raw_u": (16, 32, 256),
+    "raw_f": (16, 32, 256),
+    "split_u": (2, 512, 128),
+    "split_f": (2, 512, 128),
     "co": (2, 128, 128),
-    "cu": (2, 24) + TILE,
-    "cf": (2, 24) + TILE,
-    "px": (2, 2, 16) + TILE,
-    "rx": (2, 2, 24) + TILE,
     "u": (4, 26) + TILE,
     "f": (4, 26) + TILE,
     "kx": (4, 24) + TILE,
@@ -771,20 +761,21 @@
         s = Scratch()
         for name, ref in zip(names, scratch):
             setattr(s, name, ref)
-        s.ssem, s.rsem = scratch[len(names) :]
+        s.ssem, s.rsem, s.lsem = scratch[len(names) :]
         kernel_body(n, m, x_ref, f_ref, o_ref, s)
 
     return pl.pallas_call(
         body,
         out_shape=jax.ShapeDtypeStruct(state.shape, F32),
-        in_specs=[pl.BlockSpec(memory_space=pltpu.VMEM)] * 2,
+        in_specs=[pl.BlockSpec(memory_space=pl.ANY)] * 2,
         out_specs=pl.BlockSpec(memory_space=pltpu.VMEM),
         scratch_shapes=[pltpu.VMEM(shape, F32) for shape in SHAPES.values()]
-        + [pltpu.SemaphoreType.DMA((COPIES,))] * 2,
+        + [pltpu.SemaphoreType.DMA((COPIES,))] * 2
+        + [pltpu.SemaphoreType.DMA((2,))],
         compiler_params=pltpu.CompilerParams(
             collective_id=0, has_side_effects=True, vmem_limit_bytes=48 << 20
         ),
-    )(state, forcing)
+    )(*[pltpu.with_memory_space_constraint(v, pltpu.HBM) for v in (state, forcing)])
 
 
 def solution(mesh):

time: 65.3 us -> 54.2 us (0.83)
  Pallas kernels: 62.7 us -> 53.5 us
  local copies, waits for them, and re-layouts: 2.47 us -> 0.66 us
    pallas_call x1, Pallas kernels: 62.7 us -> 53.5 us  [on_device(): pl.pallas_call(body, out_shape=jax.ShapeDtypeStruct(state.shape, F32), in...]
    unnamed x5 -> x1, local copies, waits for them, and re-layouts: 2.47 us -> 0.66 us
where the time goes in v2:
time: 54.2 us; the launch traced here: 54.1 us
  Pallas kernels  53.5 us (99%)
  local copies, waits for them, and re-layouts  0.66 us (1%)
    pallas_call x1, Pallas kernels, on_device(): pl.pallas_call(body, out_shape=jax.ShapeDtypeStruct(state.shape, F32), in...  53.5 us

profile of v2, /device:TPU:1, one launch (start us, length us, event | category | flops | bytes accessed | tf_op | source)
XLA Modules:
  0.0 54.1 jit_solution(5453078831444333581)
XLA Ops:
  0.0 53.5 %shard_map.28 = f32[8,16,256]{2,1,0:T(8,128)S(1)} custom-call(f32[8,16,256]{2,1,0:T(8,128)} %x_ref.1, f32[8,16,256]{2,1,0:T(8,128)} %f_ref.1), custom_call_target="tpu_custom_call" | custom-call | tf_op jit(solution)/shard_map/pallas_call | solution.py:767
  53.5 0.7 %copy.4 = f32[8,16,256]{2,1,0:T(8,128)} copy(f32[8,16,256]{2,1,0:T(8,128)S(1)} %shard_map.28) | data formatting | bytes 262144

commit v3 on v2

--- a/solution.py
+++ b/solution.py
@@ -9,10 +9,12 @@
 MESH = pl.DeviceIdType.MESH
 F32 = jnp.float32
 
-AROUND = [(a, b) for a in (-1, 0, 1) for b in (-1, 0, 1) if (a, b) != (0, 0)]
+AROUND = [(-1, -1), (-1, 1), (1, -1), (1, 1), (0, -1), (0, 1), (-1, 0), (1, 0)]
 GREETED = AROUND + [(2, 0)]
-WIDE = [(a, b) for a in range(-3, 5) for b in range(-2, 3) if (a, b) != (0, 0)]
-ROUND1 = [(1, 1), (1, -1), (-1, 1), (-1, -1), (0, 1), (0, -1), (1, 0), (-1, 0)]
+WIDE = sorted(
+    [(a, b) for a in range(-3, 5) for b in range(-2, 3) if (a, b) != (0, 0)],
+    key=lambda o: -(abs(o[0]) + 2 * abs(o[1])),
+)
 FORWARD = [(0, 0, 0), (0, 0, 1), (1, 0, -1), (1, 0, 0), (1, 0, 1)] + [
     (a, 1, c) for a in (-1, 0, 1) for c in (-1, 0, 1)
 ]
@@ -87,7 +89,7 @@
     pl.semaphore_wait(barrier, len(GREETED))
     round1 = []
     number = 0
-    for a, b in ROUND1:
+    for a, b in AROUND:
         for ref, raw, hx, tx in (
             (x_ref, s.raw_u, here_x, there_x),
             (f_ref, s.raw_f, here_fx, there_fx),
@@ -116,20 +118,34 @@
     for x in range(4, 12):
         split(s.raw_u, s.split_u, x, ((8, 16),))
         split(s.raw_f, s.split_f, x, ((8, 16),))
-    for copy in round1:
+    def split_planes(planes, tiles):
+        for x in planes:
+            split(s.raw_u, s.split_u, x, tiles)
+            if 2 <= x < 13:
+                split(s.raw_f, s.split_f, x, tiles)
+
+    def collect(rows, outer):
+        for i in rows:
+            keep = inside(i - 4, (1, 8, 128), 16)[0]
+            for p in range(4):
+                at = pl.ds((p % 2) * 256 + i + 4, 8, stride=32)
+                u = s.split_u[p // 2, at, :]
+                s.u[p, i] = jnp.where(keep, u, 0.0) if outer else u
+                if 2 <= i < 22:
+                    s.f[p, i] = s.split_f[p // 2, at, :]
+
+    outside_x = (0, 1, 2, 3, 12, 13, 14, 15)
+    for copy in round1[12:16]:
         copy.wait_recv()
-    for x in range(16):
-        tiles = ((0, 8), (24, 8)) if 4 <= x < 12 else ((0, 32),)
-        split(s.raw_u, s.split_u, x, tiles)
-        if 2 <= x < 13:
-            split(s.raw_f, s.split_f, x, tiles)
-    for i in range(24):
-        keep = inside(i - 4, (1, 8, 128), 16)[0]
-        for p in range(4):
-            at = pl.ds((p % 2) * 256 + i + 4, 8, stride=32)
-            u = s.split_u[p // 2, at, :]
-            s.u[p, i] = u if 4 <= i < 20 else jnp.where(keep, u, 0.0)
-            s.f[p, i] = s.split_f[p // 2, at, :]
+    split_planes(outside_x, ((8, 16),))
+    collect(range(4, 20), False)
+    for copy in round1[8:12]:
+        copy.wait_recv()
+    split_planes(range(4, 12), ((0, 8), (24, 8)))
+    for copy in round1[0:8]:
+        copy.wait_recv()
+    split_planes(outside_x, ((0, 8), (24, 8)))
+    collect((0, 1, 2, 3, 20, 21, 22, 23), True)
     s.u[:, 24:26] = jnp.zeros((4, 2, 8, 128), F32)
 
     def faces(i, carry):
@@ -446,7 +462,7 @@
     mine = {-1: pl.ds(2, 3), 0: pl.ds(2, 4), 1: pl.ds(4, 2)}
     theirs = {-1: pl.ds(6, 3), 0: pl.ds(2, 4), 1: pl.ds(0, 2)}
     round3 = []
-    for a, b in AROUND + [(-2, -1), (-2, 0), (-2, 1)]:
+    for a, b in [(-2, -1), (-2, 1)] + AROUND + [(-2, 0)]:
         round3.append(send(s.re2.at[1, mine[b]], s.re2.at[1 - a, theirs[b]], number, a, b))
         number += 1
 
@@ -519,9 +535,9 @@
                     value = jnp.where(lane % 4 == j, other, value)
             s.ra3[2, 24 + 4 * y + q : 25 + 4 * y + q, :] = value[2:3]
 
-    def send_wide(ref, number):
+    def send_wide(ref, number, last=4):
         copies = []
-        for a, b in WIDE:
+        for a, b in [o for o in WIDE if o[0] <= last]:
             copies.append(send(ref.at[2, middle], ref.at[2 + b, pl.ds(8 * (a + 3), 8)], number, -a, -b))
             number += 1
         return copies, number
@@ -551,7 +567,7 @@
         s.rb3[2, 24 + y : 25 + y, :] = b3[2:3]
         s.rb3[2, 26 + y : 27 + y, :] = e3[2:3]
 
-    round4, number = send_wide(s.rb3, number)
+    round4, number = send_wide(s.rb3, number, 3)
     for copy in round3a:
         copy.wait_recv()
 

time: 54.2 us -> 51.5 us (0.950)
  Pallas kernels: 53.5 us -> 50.7 us
    pallas_call x1, Pallas kernels: 53.5 us -> 50.7 us  [on_device(): pl.pallas_call(body, out_shape=jax.ShapeDtypeStruct(state.shape, F32), in...]
where the time goes in v3:
time: 51.5 us; the launch traced here: 51.4 us
  Pallas kernels  50.7 us (98%)
  local copies, waits for them, and re-layouts  0.66 us (1%)
    pallas_call x1, Pallas kernels, on_device(): pl.pallas_call(body, out_shape=jax.ShapeDtypeStruct(state.shape, F32), in...  50.7 us

profile of v3, /device:TPU:1, one launch (start us, length us, event | category | flops | bytes accessed | tf_op | source)
XLA Modules:
  0.0 51.4 jit_solution(14387853533924849505)
XLA Ops:
  0.0 50.7 %shard_map.28 = f32[8,16,256]{2,1,0:T(8,128)S(1)} custom-call(f32[8,16,256]{2,1,0:T(8,128)} %x_ref.1, f32[8,16,256]{2,1,0:T(8,128)} %f_ref.1), custom_call_target="tpu_custom_call" | custom-call | tf_op jit(solution)/shard_map/pallas_call | solution.py:783
  50.7 0.7 %copy.4 = f32[8,16,256]{2,1,0:T(8,128)} copy(f32[8,16,256]{2,1,0:T(8,128)S(1)} %shard_map.28) | data formatting | bytes 262144

commit v4 on v3

--- a/solution.py
+++ b/solution.py
@@ -139,13 +139,6 @@
         copy.wait_recv()
     split_planes(outside_x, ((8, 16),))
     collect(range(4, 20), False)
-    for copy in round1[8:12]:
-        copy.wait_recv()
-    split_planes(range(4, 12), ((0, 8), (24, 8)))
-    for copy in round1[0:8]:
-        copy.wait_recv()
-    split_planes(outside_x, ((0, 8), (24, 8)))
-    collect((0, 1, 2, 3, 20, 21, 22, 23), True)
     s.u[:, 24:26] = jnp.zeros((4, 2, 8, 128), F32)
 
     def faces(i, carry):
@@ -187,7 +180,6 @@
             s.h[k, at] = value
         return carry
 
-    lax.fori_loop(0, 12, faces, 0, unroll=True)
 
     def beside(ref, row, k):
         at = pl.ds(row, k)
@@ -238,7 +230,6 @@
                 s.e0[p, at] = jnp.where(keep, weight * newton, 0.0)
         return carry
 
-    lax.fori_loop(0, 10, smooth0, 0, unroll=True)
 
     def residual0(i, carry):
         row = 3 + 2 * i
@@ -250,7 +241,20 @@
         s.r0[at] = jnp.where(keep, r[0] + 0.5 * (r[1] + xsh(r[1], -1)), 0.0)
         return carry
 
-    lax.fori_loop(0, 9, residual0, 0, unroll=True)
+    def stretch(parts):
+        for step, low, high in parts:
+            lax.fori_loop(low, high, step, 0, unroll=True)
+
+    stretch(((faces, 2, 9), (smooth0, 2, 8), (residual0, 2, 7)))
+    for copy in round1[8:12]:
+        copy.wait_recv()
+    split_planes(range(4, 12), ((0, 8), (24, 8)))
+    for copy in round1[0:8]:
+        copy.wait_recv()
+    split_planes(outside_x, ((0, 8), (24, 8)))
+    collect((0, 1, 2, 3, 20, 21, 22, 23), True)
+    stretch(((faces, 0, 2), (faces, 9, 12), (smooth0, 0, 2), (smooth0, 8, 10)))
+    stretch(((residual0, 0, 2), (residual0, 7, 9)))
 
     def level1(i, only_up):
         base = 2 * i
@@ -301,20 +305,21 @@
             return s.a1[at, pl.ds(row, k)]
         return s.a1[9 + at, pl.ds(row if b == 1 else row - 1, k)]
 
-    level1(0, True)
-
-    def level1_step(i, carry):
-        level1(i, False)
-        return carry
-
-    lax.fori_loop(1, 11, level1_step, 0, unroll=True)
-
     sub = iota((8, 128), 0)
 
     def start1(y, carry):
         row = 4 + 2 * y
         b1 = s.r0[row] + 0.5 * (s.r0[row - 1] + s.r0[row + 1])
-        e1 = s.w1[y + 2] * b1
+        fine = row
+
+        def mass(k):
+            return s.g[k, fine] + 0.25 * (s.g[k, fine + 1] + s.g[k, fine - 1])
+
+        sx0 = mass(0)
+        below = 0.25 * (s.h[0, fine - 2] + s.h[0, fine - 1])
+        below = jnp.where((gy == 0) & (y == 0), s.h[0, fine - 1], below)
+        above = 0.25 * (s.h[0, fine] + s.h[0, fine + 1])
+        e1 = WEIGHT * b1 / (sx0 + xsh(sx0, -1) + mass(4) + above + below)
         s.re1[1, y + 2] = jnp.where(sub < 4, pltpu.roll(e1, 6, 0), pltpu.roll(b1, 2, 0))
         return carry
 
@@ -326,6 +331,14 @@
     for a, b in AROUND:
         round2.append(send(s.re1.at[1, mine[b]], s.re1.at[1 - a, theirs[b]], number, a, b))
         number += 1
+
+    level1(0, True)
+
+    def level1_step(i, carry):
+        level1(i, False)
+        return carry
+
+    lax.fori_loop(1, 11, level1_step, 0, unroll=True)
 
     def coarsen(coefficient, row, d, store):
         def get(o, r):
@@ -617,6 +630,8 @@
         s.re3[2, 24 + y : 25 + y, :] = s.e3[1, 4 + y, 3:4, :]
 
     round5, number = send_wide(s.re3, number)
+    for copy in started:
+        copy.wait_send()
     for copy in round5:
         copy.wait_recv()
     for dy in range(5):
@@ -713,8 +728,6 @@
         va, vb = jnp.where(low, even, odd), pltpu.roll(jnp.where(low, odd, even), 64, 1)
         o_ref[x, :, 0:128] = jnp.take_along_axis(va, take, axis=1, mode="promise_in_bounds")
         o_ref[x, :, 128:256] = jnp.take_along_axis(vb, take, axis=1, mode="promise_in_bounds")
-    for copy in started:
-        copy.wait_send()
 
 
 COPIES = 16 + 8 + 11 + 11 + 3 * len(WIDE)

time: 51.5 us -> 49.7 us (0.965)
  Pallas kernels: 50.7 us -> 48.9 us
    pallas_call x1, Pallas kernels: 50.7 us -> 48.9 us  [on_device(): pl.pallas_call(body, out_shape=jax.ShapeDtypeStruct(state.shape, F32), in...]
where the time goes in v4:
time: 49.7 us; the launch traced here: 49.6 us
  Pallas kernels  48.9 us (98%)
  local copies, waits for them, and re-layouts  0.66 us (1%)
    pallas_call x1, Pallas kernels, on_device(): pl.pallas_call(body, out_shape=jax.ShapeDtypeStruct(state.shape, F32), in...  48.9 us

profile of v4, /device:TPU:1, one launch (start us, length us, event | category | flops | bytes accessed | tf_op | source)
XLA Modules:
  0.0 49.6 jit_solution(1194889777912608163)
XLA Ops:
  0.0 48.9 %shard_map.28 = f32[8,16,256]{2,1,0:T(8,128)S(1)} custom-call(f32[8,16,256]{2,1,0:T(8,128)} %x_ref.1, f32[8,16,256]{2,1,0:T(8,128)} %f_ref.1), custom_call_target="tpu_custom_call" | custom-call | tf_op jit(solution)/shard_map/pallas_call | solution.py:796
  48.9 0.7 %copy.4 = f32[8,16,256]{2,1,0:T(8,128)} copy(f32[8,16,256]{2,1,0:T(8,128)S(1)} %shard_map.28) | data formatting | bytes 262144

commit v5 on v4

--- a/solution.py
+++ b/solution.py
@@ -538,7 +538,6 @@
 
     lax.fori_loop(0, 2, coarsen2, 0, unroll=True)
     lane = iota((8, 128), 1)
-    middle = pl.ds(24, 8)
     for y in range(2):
         for q in range(4):
             value = s.a3own[4 * q, y]
@@ -548,14 +547,14 @@
                     value = jnp.where(lane % 4 == j, other, value)
             s.ra3[2, 24 + 4 * y + q : 25 + 4 * y + q, :] = value[2:3]
 
-    def send_wide(ref, number, last=4):
+    def send_wide(ref, number, last, rows):
         copies = []
         for a, b in [o for o in WIDE if o[0] <= last]:
-            copies.append(send(ref.at[2, middle], ref.at[2 + b, pl.ds(8 * (a + 3), 8)], number, -a, -b))
+            copies.append(send(ref.at[2, pl.ds(24, rows)], ref.at[2 + b, pl.ds(8 * (a + 3), rows)], number, -a, -b))
             number += 1
         return copies, number
 
-    round3a, number = send_wide(s.ra3, number)
+    round3a, number = send_wide(s.ra3, number, 4, 8)
 
     for copy in round3:
         copy.wait_recv()
@@ -580,7 +579,7 @@
         s.rb3[2, 24 + y : 25 + y, :] = b3[2:3]
         s.rb3[2, 26 + y : 27 + y, :] = e3[2:3]
 
-    round4, number = send_wide(s.rb3, number, 3)
+    round4, number = send_wide(s.rb3, number, 3, 4)
     for copy in round3a:
         copy.wait_recv()
 
@@ -629,7 +628,7 @@
     for y in range(2):
         s.re3[2, 24 + y : 25 + y, :] = s.e3[1, 4 + y, 3:4, :]
 
-    round5, number = send_wide(s.re3, number)
+    round5, number = send_wide(s.re3, number, 4, 2)
     for copy in started:
         copy.wait_send()
     for copy in round5:

time: 49.7 us -> 49.2 us (0.990)
  Pallas kernels: 48.9 us -> 48.4 us
    pallas_call x1, Pallas kernels: 48.9 us -> 48.4 us  [on_device(): pl.pallas_call(body, out_shape=jax.ShapeDtypeStruct(state.shape, F32), in...]
where the time goes in v5:
time: 49.2 us; the launch traced here: 49.1 us
  Pallas kernels  48.4 us (98%)
  local copies, waits for them, and re-layouts  0.66 us (1%)
    pallas_call x1, Pallas kernels, on_device(): pl.pallas_call(body, out_shape=jax.ShapeDtypeStruct(state.shape, F32), in...  48.4 us

profile of v5, /device:TPU:1, one launch (start us, length us, event | category | flops | bytes accessed | tf_op | source)
XLA Modules:
  0.0 49.1 jit_solution(381316449249952)
XLA Ops:
  0.0 48.4 %shard_map.28 = f32[8,16,256]{2,1,0:T(8,128)S(1)} custom-call(f32[8,16,256]{2,1,0:T(8,128)} %x_ref.1, f32[8,16,256]{2,1,0:T(8,128)} %f_ref.1), custom_call_target="tpu_custom_call" | custom-call | tf_op jit(solution)/shard_map/pallas_call | solution.py:795
  48.4 0.7 %copy.4 = f32[8,16,256]{2,1,0:T(8,128)} copy(f32[8,16,256]{2,1,0:T(8,128)S(1)} %shard_map.28) | data formatting | bytes 262144
